TPU v7x, 256 devices: a whole 4x4x8 slice. The times are simulated.
256 devices in a mesh: expert: 128 (over y, z, x), half: 2 (over core).
Axes of the slice: x: 4, y: 4, z: 8, core: 2. Of those that a mesh axis runs over, the one named last changes fastest.
Arguments:
- tokens: bfloat16 [8192, 2048], P('expert'), may hold values from -6 to 6
- cotangent: bfloat16 [8192, 2048], P('expert'), may hold values from -1 to 1
- expert_ids: int32 [8192, 8], P('expert'), may hold values from 0 to 127, all different within a row; in each aligned block of 64 rows (0 to 63, 64 to 127, ...) at most 6 rows name the same one
- gate_weights: float32 [8192, 8], P('expert'), may hold values from 0.1 to 0.6
- w_gate: bfloat16 [128, 2048, 768], P('expert', None, 'half'), may hold values from -0.125 to 0.125
- w_up: bfloat16 [128, 2048, 768], P('expert', None, 'half'), may hold values from -0.125 to 0.125
- w_down: bfloat16 [128, 768, 2048], P('expert', 'half'), may hold values from -0.21875 to 0.21875
Outputs:
- input_grad: bfloat16 [8192, 2048], P('expert')
- gate_grad: bfloat16 [8192, 8], P('expert')
Inputs may be any that keep to these rules, and one draw needn't show every extreme that they name: `expert_ids`: each token names 8 different experts. Among the 64 tokens of one index of expert, no expert is named by more than 6 tokens, a bound that some block reaches; every expert is named somewhere.
All inputs are finite; a program needn't handle non-finite values.
Results may differ from a plain program's by a relative error of at most 0.0085.
Values may be sent and summed in bfloat16 or wider, within the bound.
A program may use at most 64 MiB of HBM per device.

v0:
```python
import jax
import jax.numpy as jnp
from jax import lax
from jax.sharding import PartitionSpec as P


def expert_terms(rows, grads, gate_one, up_one, down_one):
    gate_pre = jnp.einsum("ncd,df->ncf", rows, gate_one, preferred_element_type=jnp.float32)
    up_pre = jnp.einsum("ncd,df->ncf", rows, up_one, preferred_element_type=jnp.float32)
    grad_hidden = jnp.einsum("ncd,fd->ncf", grads, down_one, preferred_element_type=jnp.float32)
    sigmoid_gate = jax.nn.sigmoid(gate_pre)
    silu_gate = gate_pre * sigmoid_gate
    scores = jnp.sum(grad_hidden * silu_gate * up_pre, axis=-1)
    grad_up = (grad_hidden * silu_gate).astype(jnp.bfloat16)
    grad_gate = (
        grad_hidden * up_pre * sigmoid_gate * (1.0 + gate_pre * (1.0 - sigmoid_gate))
    ).astype(jnp.bfloat16)
    input_part = jnp.einsum("ncf,df->ncd", grad_gate, gate_one, preferred_element_type=jnp.float32)
    input_part = input_part + jnp.einsum(
        "ncf,df->ncd", grad_up, up_one, preferred_element_type=jnp.float32
    )
    return (input_part, scores)


def owner_sum(back, slot_index, gate_weights):
    width = back.shape[2]
    picked = back.reshape(-1, width)[slot_index]
    picked = picked.reshape(gate_weights.shape[0], gate_weights.shape[1], width)
    return jnp.einsum(
        "tk,tkw->tw", gate_weights, picked, preferred_element_type=jnp.float32
    ).astype(jnp.bfloat16)


def per_device(tokens, cotangent, expert_ids, gate_weights, w_gate, w_up, w_down):
    tok_count, top_count = expert_ids.shape
    experts = lax.axis_size("expert")
    capacity = 3 * tok_count * top_count // (2 * experts)
    routed = expert_ids.reshape(-1)
    onehot = (routed[:, None] == jnp.arange(experts, dtype=jnp.int32)[None, :]).astype(jnp.int32)
    earlier = jnp.cumsum(onehot, axis=0) - onehot
    slot_index = routed * capacity + jnp.sum(earlier * onehot, axis=1)
    owner_rows = jnp.arange(tok_count * top_count, dtype=jnp.int32) // top_count + 1
    slot_token = jnp.zeros((experts * capacity,), jnp.int32).at[slot_index].set(owner_rows)
    slot_live = (slot_token > 0)[:, None]
    picked = jnp.maximum(slot_token - 1, 0)
    sent_tokens = jnp.where(slot_live, tokens[picked], jnp.zeros((), tokens.dtype)).reshape(
        experts, capacity, -1
    )
    sent_grads = jnp.where(slot_live, cotangent[picked], jnp.zeros((), cotangent.dtype)).reshape(
        experts, capacity, -1
    )
    gate_one = w_gate[0]
    up_one = w_up[0]
    down_one = w_down[0]
    rows = lax.all_to_all(sent_tokens, "expert", split_axis=0, concat_axis=0, tiled=True)
    grads = lax.all_to_all(sent_grads, "expert", split_axis=0, concat_axis=0, tiled=True)
    input_part, scores = expert_terms(rows, grads, gate_one, up_one, down_one)
    input_half = lax.psum_scatter(input_part, "half", scatter_dimension=2, tiled=True).astype(
        jnp.bfloat16
    )
    scores = lax.psum(scores, "half").astype(jnp.bfloat16)
    input_full = lax.all_gather(input_half, "half", axis=2, tiled=True)
    back, back_scores = (
        lax.all_to_all(input_full, "expert", split_axis=0, concat_axis=0, tiled=True),
        lax.all_to_all(scores, "expert", split_axis=0, concat_axis=0, tiled=True),
    )
    input_grad = owner_sum(back, slot_index, gate_weights)
    gate_grad = back_scores.reshape(-1)[slot_index].reshape(tok_count, top_count)
    return (input_grad, gate_grad)


def solution(mesh):
    placed = (
        P("expert", None),
        P("expert", None),
        P("expert", None),
        P("expert", None),
        P("expert", None, "half"),
        P("expert", None, "half"),
        P("expert", "half", None),
    )
    return jax.shard_map(
        per_device,
        mesh=mesh,
        in_specs=placed,
        out_specs=(P("expert", None), P("expert", None)),
        check_vma=False,
    )
```

profile of v0, /device:TPU:1, one launch (start us, length us, event | category | flops | bytes accessed | tf_op | source)
XLA Modules:
  0.0 449.5 jit_solution(11026966372310681473)
XLA Ops:
  7.2 0.0 copy-start
  7.2 0.0 copy-start.1
  7.2 0.8 broadcast_multiply_fusion
  8.0 0.8 copy.20
  8.8 0.1 eq.29
  8.9 0.1 eq.25
  9.0 0.1 copy.19
  9.1 0.1 mul.43
  9.2 0.1 copy.22
  9.3 0.2 fusion.18
  9.6 0.2 fusion.17
  9.8 2.4 scatter_custom_fusion
  12.3 0.2 broadcast_in_dim.27
  12.5 0.0 copy-done.1
  12.5 4.3 gather_fusion.1
  16.8 0.0 copy-start.2
  16.8 6.3 %gather.19 = bf16[128,6,2048]{2,1,0:T(8,128)(2,1)} reshape(bf16[768,2048]{1,0:T(8,128)(2,1)} %gather_fusion.1) | data formatting | bytes 6291456 | tf_op jit(solution)/shard_map/gather | solution.py:46
  23.1 0.0 copy-done.2
  23.1 4.3 gather_fusion
  27.4 6.3 %gather.17 = bf16[128,6,2048]{2,1,0:T(8,128)(2,1)} reshape(bf16[768,2048]{1,0:T(8,128)(2,1)} %gather_fusion) | data formatting | bytes 6291456 | tf_op jit(solution)/shard_map/gather | solution.py:49
  33.7 5.2 %broadcast_select_fusion.1 = (bf16[128,6,2048]{2,1,0:T(8,128)(2,1)S(1)}, bf16[128,6,2048]{2,1,0:T(8,128)(2,1)}) fusion(bf16[128,6,2048]{2,1,0:T(8,128)(2,1)} %gather.17, pred[128,6]{1,0:T(8,128)(4,1)S(1)} %broadcast_in_dim.27, bf16[128,6,2048]{2,1,0:T(8,128)(2,1)} %gather.19), kind=kLoop, calls=%fused_computation.6 | loop fusion | flops 3145728 | bytes 12583680 | tf_op jit(solution)/shard_map/jit(_where)/select_n | solution.py:49
  38.9 109.5 %all_to_all.24 = bf16[128,6,2048]{2,1,0:T(8,128)(2,1)} all-to-all(bf16[128,6,2048]{2,1,0:T(8,128)(2,1)S(1)} %get-tuple-element.6), channel_id=1, replica_groups=mesh['expert'=128,'half'=2] {'expert'}, dimensions={0} | all-to-all | bytes 6291456 | tf_op jit(solution)/shard_map/all_to_all | solution.py:56
  148.4 11.1 %all-to-all-start.1 = ((bf16[128,6,2048]{2,1,0:T(8,128)(2,1)}), bf16[128,6,2048]{2,1,0:T(8,128)(2,1)}, u32[]{:S(2)}, u32[]{:S(2)}) async-start(bf16[128,6,2048]{2,1,0:T(8,128)(2,1)} %get-tuple-element.7), calls=%async_computation.1 | async-start | bytes 8388608 | tf_op jit(solution)/shard_map/all_to_all | solution.py:55
  159.5 0.2 reduce-scatter.2.cloned.1.call-start
  159.8 6.3 %fusion = f32[128,6,384]{2,0,1:T(8,128)S(1)} fusion(bf16[128,6,2048]{2,1,0:T(8,128)(2,1)} %all_to_all.24, bf16[1,384,2048]{2,1,0:T(8,128)(2,1)} %param.13), kind=kOutput, calls=%fused_computation.8 | convolution fusion | flops 1207959552 | bytes 5898240 | tf_op jit(solution)/shard_map/ncd,fd->ncf/dot_general | solution.py:10
  166.1 86.2 %all-to-all-done.1 = bf16[128,6,2048]{2,1,0:T(8,128)(2,1)} async-done(((bf16[128,6,2048]{2,1,0:T(8,128)(2,1)}), bf16[128,6,2048]{2,1,0:T(8,128)(2,1)}, u32[]{:S(2)}, u32[]{:S(2)}) %all-to-all-start.1) | async-done | bytes 3145760 | tf_op jit(solution)/shard_map/all_to_all | solution.py:55
  252.2 6.2 %fusion.2 = f32[128,6,384]{2,0,1:T(8,128)S(1)} fusion(bf16[128,6,2048]{2,1,0:T(8,128)(2,1)} %all-to-all-done.1, bf16[1,2048,384]{2,1,0:T(8,128)(2,1)} %param.11), kind=kOutput, calls=%fused_computation.10 | convolution fusion | flops 1207959552 | bytes 5898240 | tf_op jit(solution)/shard_map/ncd,df->ncf/dot_general | solution.py:8
  258.4 0.0 copy-done
  258.4 0.0 copy-start.3
  258.4 6.1 %multiply_reduce_fusion = (f32[128,6]{0,1:T(8,128)S(1)}, f32[128,6,384]{2,0,1:T(8,128)S(1)}) fusion(f32[128,6,384]{2,0,1:T(8,128)S(1)} %fusion, f32[128,6,384]{2,0,1:T(8,128)S(1)} %fusion.2, bf16[1,2048,384]{2,1,0:T(8,128)(2,1)S(1)} %copy-done, bf16[128,6,2048]{2,1,0:T(8,128)(2,1)} %all-to-all-done.1), kind=kOutput, calls=%fused_computation.22 | convolution fusion | flops 1210023168 | bytes 8260608 | tf_op jit(solution)/shard_map/ncd,df->ncf/dot_general | solution.py:9
  264.5 0.0 copy-done.3
  264.5 2.3 fusion.8
  266.8 4.6 %convolution_add_fusion = f32[128,6,2048]{2,0,1:T(8,128)} fusion(f32[128,6,2048]{2,0,1:T(8,128)S(1)} %fusion.8, bf16[1,2048,384]{2,1,0:T(8,128)(2,1)S(1)} %copy-done, f32[128,6,384]{2,0,1:T(8,128)S(1)} %fusion, f32[128,6,384]{2,0,1:T(8,128)S(1)} %fusion.2), kind=kOutput, calls=%fused_computation.7 | convolution fusion | flops 1211301888 | bytes 16515072 | tf_op jit(solution)/shard_map/ncf,df->ncd/dot_general | solution.py:19
  271.3 0.0 reduce-scatter.2.cloned.1.call-update
  271.4 0.0 all-gather.2.cloned.1.call-start
  271.4 18.8 %reduce-scatter.2.cloned.1.call-done = f32[128,6,1024]{2,0,1:T(8,128)} async-done(((f32[128,6,2048]{2,0,1:T(8,128)}), f32[128,6,1024]{2,0,1:T(8,128)}) %reduce-scatter.2.cloned.1.call-update) | async-done | bytes 3145744 | tf_op jit(solution)/shard_map/reduce_scatter | solution.py:58
  290.2 3.3 convert_element_type.26
  293.5 0.0 all-gather.2.cloned.1.call-update
  293.5 2.6 psum.7
  296.1 0.8 copy.28
  296.8 13.6 %all-to-all-start.3 = ((bf16[128,1,6]{2,1,0:T(2,128)(2,1)}), bf16[128,1,6]{2,1,0:T(2,128)(2,1)S(1)}, u32[]{:S(2)}, u32[]{:S(2)}) async-start(bf16[128,1,6]{2,1,0:T(2,128)(2,1)} %copy.28), calls=%async_computation.4 | async-start | bytes 131072 | tf_op jit(solution)/shard_map/all_to_all | solution.py:65
  310.4 2.2 all-gather.2.cloned.1.call-done
  312.6 5.6 %copy.27 = bf16[128,6,2048]{2,1,0:T(8,128)(2,1)} copy(bf16[128,6,2048]{2,0,1:T(8,128)(2,1)} %all-gather.2.cloned.1.call-done) | data formatting | bytes 6291456 | tf_op jit(solution)/shard_map/all_gather | solution.py:62
  318.2 0.0 copy-start.4
  318.2 2.7 all-to-all-done.3
  320.9 11.8 %all-to-all-start.2 = ((bf16[128,6,2048]{2,1,0:T(8,128)(2,1)}), bf16[128,6,2048]{2,1,0:T(8,128)(2,1)}, u32[]{:S(2)}, u32[]{:S(2)}) async-start(bf16[128,6,2048]{2,1,0:T(8,128)(2,1)} %copy.27), calls=%async_computation.3 | async-start | bytes 8388608 | tf_op jit(solution)/shard_map/all_to_all | solution.py:64
  332.7 0.0 copy-done.4
  332.7 0.1 copy.30
  332.9 0.2 reduce
  333.0 0.1 reshape.82
  333.2 3.5 gather_fusion.3
  336.7 0.1 reshape.83
  336.8 0.7 copy.29
  337.5 88.1 %all-to-all-done.2 = bf16[128,6,2048]{2,1,0:T(8,128)(2,1)} async-done(((bf16[128,6,2048]{2,1,0:T(8,128)(2,1)}), bf16[128,6,2048]{2,1,0:T(8,128)(2,1)}, u32[]{:S(2)}, u32[]{:S(2)}) %all-to-all-start.2) | async-done | bytes 3145760 | tf_op jit(solution)/shard_map/all_to_all | solution.py:64
  425.6 6.3 %reshape.80 = bf16[768,2048]{1,0:T(8,128)(2,1)} reshape(bf16[128,6,2048]{2,1,0:T(8,128)(2,1)} %all-to-all-done.2) | data formatting | bytes 6291456 | tf_op jit(solution)/shard_map/reshape | solution.py:27
  431.9 7.6 %gather_fusion.2 = bf16[512,2048]{1,0:T(8,128)(2,1)} fusion(bf16[768,2048]{1,0:T(8,128)(2,1)} %reshape.80, s32[1024]{0:T(1024)S(1)} %pad_clamp_fusion), kind=kCustom, calls=%fused_computation.2 | custom fusion | bytes 4196352 | tf_op jit(solution)/shard_map/gather | solution.py:27
  439.5 2.3 fusion.6
  441.8 0.9 copy.41
  (12 shorter events, 0.1 us)
Async XLA Ops:
  7.2 251.2 %copy-start = (bf16[1,2048,384]{2,1,0:T(8,128)(2,1)S(1)}, bf16[1,2048,384]{2,1,0:T(8,128)(2,1)}, u32[]{:S(2)}) copy-start(bf16[1,2048,384]{2,1,0:T(8,128)(2,1)} %param.12) | copy-start | bytes 4718596
  7.2 5.3 %copy-start.1 = (bf16[64,2048]{1,0:T(8,128)(2,1)S(1)}, bf16[64,2048]{1,0:T(8,128)(2,1)}, u32[]{:S(2)}) copy-start(bf16[64,2048]{1,0:T(8,128)(2,1)} %param.7) | copy-start | bytes 786436
  16.8 6.3 %copy-start.2 = (bf16[64,2048]{1,0:T(8,128)(2,1)S(1)}, bf16[64,2048]{1,0:T(8,128)(2,1)}, u32[]{:S(2)}) copy-start(bf16[64,2048]{1,0:T(8,128)(2,1)} %param.8) | copy-start | bytes 786436
  148.4 103.8 %all-to-all-start.1 = ((bf16[128,6,2048]{2,1,0:T(8,128)(2,1)}), bf16[128,6,2048]{2,1,0:T(8,128)(2,1)}, u32[]{:S(2)}, u32[]{:S(2)}) async-start(bf16[128,6,2048]{2,1,0:T(8,128)(2,1)} %get-tuple-element.7), calls=%async_computation.1 | async-start | bytes 8388608 | tf_op jit(solution)/shard_map/all_to_all | solution.py:55
  159.5 130.7 %reduce-scatter.2.cloned.1.call-start = ((), (), s32[]{:S(2)}) async-start(), calls=%async_computation.5 | async-start | bytes 9437184 | tf_op jit(solution)/shard_map/reduce_scatter | solution.py:58
  258.4 6.1 %copy-start.3 = (bf16[1,2048,384]{2,1,0:T(8,128)(2,1)S(1)}, bf16[1,2048,384]{2,1,0:T(8,128)(2,1)}, u32[]{:S(2)}) copy-start(bf16[1,2048,384]{2,1,0:T(8,128)(2,1)} %param.11) | copy-start | bytes 4718596
  271.4 41.2 %all-gather.2.cloned.1.call-start = ((), (), s32[]{:S(2)}) async-start(), calls=%async_computation.6 | async-start | bytes 4718592 | tf_op jit(solution)/shard_map/all_gather | solution.py:62
  296.8 24.1 %all-to-all-start.3 = ((bf16[128,1,6]{2,1,0:T(2,128)(2,1)}), bf16[128,1,6]{2,1,0:T(2,128)(2,1)S(1)}, u32[]{:S(2)}, u32[]{:S(2)}) async-start(bf16[128,1,6]{2,1,0:T(2,128)(2,1)} %copy.28), calls=%async_computation.4 | async-start | bytes 131072 | tf_op jit(solution)/shard_map/all_to_all | solution.py:65
  318.2 14.5 %copy-start.4 = (f32[64,8]{0,1:T(8,128)S(1)}, f32[64,8]{0,1:T(8,128)}, u32[]{:S(2)}) copy-start(f32[64,8]{0,1:T(8,128)} %param.10) | copy-start | bytes 6148
  320.9 104.6 %all-to-all-start.2 = ((bf16[128,6,2048]{2,1,0:T(8,128)(2,1)}), bf16[128,6,2048]{2,1,0:T(8,128)(2,1)}, u32[]{:S(2)}, u32[]{:S(2)}) async-start(bf16[128,6,2048]{2,1,0:T(8,128)(2,1)} %copy.27), calls=%async_computation.3 | async-start | bytes 8388608 | tf_op jit(solution)/shard_map/all_to_all | solution.py:64
Sparse Core Ops, SparseCore 0:
  271.5 18.6 reduce-scatter.1
  293.6 18.9 all-gather.1
where the time goes:
time: 453 us; the launch traced here: 449 us
  waiting for transfers between devices  198 us (44%)
  blocking collectives  112 us (25%)
  local copies, waits for them, and re-layouts  50.7 us (11%)
  starting transfers between devices  36.7 us (8%)
  matrix products  27.6 us (6%)
  between operations  14.2 us (3%)
  other arithmetic  10.1 us (2%)
    all_to_all x1, blocking collectives, per_device(): lax.all_to_all(sent_grads, 'expert', split_axis=0, concat_axis=0, tiled=T...  110 us
    all_to_all x1, waiting for transfers between devices, per_device(): lax.all_to_all(input_full, 'expert', split_axis=0, concat_axis=0, tiled=T...  88.1 us
    all_to_all x1, waiting for transfers between devices, per_device(): lax.all_to_all(sent_tokens, 'expert', split_axis=0, concat_axis=0, tiled=...  86.2 us
    reduce_scatter x1, waiting for transfers between devices, per_device(): lax.psum_scatter(input_part, 'half', scatter_dimension=2, tiled=True)  18.8 us
    all_to_all x1, starting transfers between devices, per_device(): lax.all_to_all(scores, 'expert', split_axis=0, concat_axis=0, tiled=True)  13.6 us
    all_to_all x1, starting transfers between devices, per_device(): lax.all_to_all(input_full, 'expert', split_axis=0, concat_axis=0, tiled=T...  11.8 us
    all_to_all x1, starting transfers between devices, per_device(): lax.all_to_all(sent_tokens, 'expert', split_axis=0, concat_axis=0, tiled=...  11.1 us
    gather x2, local copies, waits for them, and re-layouts, per_device(): cotangent[picked]  10.6 us
  transfers between devices with their start and end apart: 5, of which 5 were waited for; matrix products, arithmetic and copies ran while one was open for 4% of the time, Pallas kernels for 0%

commit v1 on v0

v1 whole, which is shorter than its diff:
```python
import functools

import jax
import jax.numpy as jnp
from jax import lax
from jax.experimental import pallas as pl
from jax.experimental.pallas import tpu as pltpu
from jax.sharding import PartitionSpec as P

MESH = pl.DeviceIdType.MESH
F32 = jnp.float32
BF16 = jnp.bfloat16
NY, NZ, NX = 4, 8, 4
CAP = 6
LANES = 128


def nt(a, b):
    return lax.dot_general(a, b, (((1,), (1,)), ((), ())), preferred_element_type=F32)


def nn(a, b):
    return jnp.dot(a, b, preferred_element_type=F32)


class Sizes:
    def __init__(self, tok, dim, half_ff, top, ny, nz, nx, chunks):
        self.tok, self.dim, self.hf, self.ff, self.top = tok, dim, half_ff, 2 * half_ff, top
        self.ny, self.nz, self.nx, self.nq = ny, nz, nx, chunks
        self.xy = ny * nx
        self.src = self.xy // 2
        self.slots = CAP * nz
        self.dc = dim // chunks
        self.rows = self.src * self.slots
        self.all_slots = self.xy * self.slots
        self.col = nz * tok
        self.dh = dim // 2
        self.rc = self.dh // 2


def kernel(
    g, raw_ref, ids_ref, tok_hbm, cot_hbm, wg_hbm, wu_hbm, wd_hbm, out_ref, gate_ref,
    xall, rawall, pick, scaled, pick_t, scaled_t, sbuf, rbuf, wg, wu, wd, gacc, uacc, hacc, gg, gu,
    ret0, ret1, back0, back1, part0, part1, rsend0, rsend1, rrecv0, rrecv1,
    own_sem, w_own_sem, w_send, w_recv, raw_send, raw_recv, z_send, z_recv, xy_send, xy_recv,
    ret_send, ret_recv, rs_send, rs_recv, out_send, out_recv,
):
    e = lax.axis_index("expert")
    c = lax.axis_index("half")
    x = lax.rem(e, g.nx)
    z = lax.rem(e // g.nx, g.nz)
    y = e // (g.nx * g.nz)
    other = 1 - c
    parity = lax.rem(x + y, 2)

    def chip(yy, zz, xx):
        return (yy * g.nz + zz) * g.nx + xx

    def zmod(v):
        return lax.rem(v + 2 * g.nz, g.nz)

    def own_copy(q, src):
        return pltpu.make_async_copy(src.at[:, pl.ds(q * g.dc, g.dc)], xall.at[q, z], own_sem.at[q])

    for q in range(g.nq):
        @pl.when(c == 0)
        def _():
            own_copy(q, tok_hbm).start()

        @pl.when(c == 1)
        def _():
            own_copy(q, cot_hbm).start()

    cut = pl.ds(pl.multiple_of(c * g.hf, LANES), g.hf)
    places = (wg.at[:, cut], wu.at[:, cut], wd.at[cut, :])
    weights = (wg_hbm.at[0], wu_hbm.at[0], wd_hbm.at[0])

    def weight_own(i):
        return pltpu.make_async_copy(weights[i], places[i], w_own_sem.at[i])

    def weight_swap(i):
        return pltpu.make_async_remote_copy(
            places[i], places[i], w_send.at[i], w_recv.at[i], device_id=(e, other), device_id_type=MESH
        )

    for i in range(3):
        weight_own(i).start()
    rawall[z] = raw_ref[...]

    barrier = pltpu.get_barrier_semaphore()
    for dy in range(g.ny):
        for dx in range(g.nx):
            peer = chip(lax.rem(y + dy, g.ny), z, lax.rem(x + dx, g.nx))
            if dy or dx:
                pl.semaphore_signal(barrier, inc=1, device_id=(peer, c), device_id_type=MESH)
            pl.semaphore_signal(barrier, inc=1, device_id=(peer, other), device_id_type=MESH)
    for dz in range(1, g.nz):
        pl.semaphore_signal(barrier, inc=1, device_id=(chip(y, zmod(z + dz), x), c), device_id_type=MESH)
    pl.semaphore_wait(barrier, 2 * g.xy - 1 + g.nz - 1)

    def raw_copy(dz):
        return pltpu.make_async_remote_copy(
            rawall.at[z], rawall.at[z], raw_send.at[dz - 1], raw_recv.at[dz - 1],
            device_id=(chip(y, zmod(z + dz), x), c), device_id_type=MESH,
        )

    for dz in range(1, g.nz):
        raw_copy(dz).start()

    def hops(q, way):
        return g.nz // 2 if (q + way) % 2 == 0 else g.nz // 2 - 1

    def z_copy(q, way, step):
        sign = 1 - 2 * way
        block = zmod(z - sign * (step - 1))
        return pltpu.make_async_remote_copy(
            xall.at[q, block], xall.at[q, block], z_send.at[q, way, step - 1], z_recv.at[q, way, step - 1],
            device_id=(chip(y, zmod(z + sign), x), c), device_id_type=MESH,
        )

    for q in range(g.nq):
        own_copy(q, tok_hbm).wait()
    for q in range(2):
        for way in range(2):
            z_copy(q, way, 1).start()
    for i in range(3):
        weight_own(i).wait()
        weight_swap(i).start()

    for dz in range(1, g.nz):
        raw_copy(dz).wait_recv()
    lane = lax.broadcasted_iota(jnp.int32, (16, LANES), 1)
    pairs = [
        jnp.where(lane < g.tok, rawall[2 * p], rawall[2 * p + 1]) for p in range(g.nz // 2)
    ]
    raw = jnp.concatenate(pairs, axis=1)
    place = lax.broadcasted_iota(jnp.int32, (g.xy, g.col), 0)
    named_by = (((place // g.nx) * g.nz + z) * g.nx + lax.rem(place, g.nx)).astype(F32)
    named = jnp.zeros((g.xy, g.col), F32)
    weight = jnp.zeros((g.xy, g.col), F32)
    for k in range(g.top):
        hit = raw[k:k + 1, :] == named_by
        named = named + jnp.where(hit, 1.0, 0.0)
        weight = weight + jnp.where(hit, raw[8 + k:9 + k, :], 0.0)
    early = lax.broadcasted_iota(jnp.int32, (g.col, g.col), 0)
    late = lax.broadcasted_iota(jnp.int32, (g.col, g.col), 1)
    before = jnp.where((early // g.tok == late // g.tok) & (early < late), 1.0, 0.0).astype(BF16)
    rank = nn(named.astype(BF16), before)
    token = lax.broadcasted_iota(jnp.int32, (g.xy, g.col), 1)
    key = jnp.where(named > 0.0, rank + (CAP * (token // g.tok)).astype(F32), -1.0)
    slot = lax.broadcasted_iota(jnp.int32, (g.slots, g.col), 0).astype(F32)
    for d in range(g.xy):
        hit = key[d:d + 1, :] == slot
        pick[d * g.slots:(d + 1) * g.slots, :] = jnp.where(hit, 1.0, 0.0).astype(BF16)
        scaled[d * g.slots:(d + 1) * g.slots, :] = jnp.where(hit, weight[d:d + 1, :], 0.0).astype(BF16)

    mine = y * (g.nx // 2) + x // 2

    def to_plane(q, off, do):
        yy = lax.rem(y + off // g.nx, g.ny)
        xx = lax.rem(x + lax.rem(off, g.nx), g.nx)
        there = yy * g.nx + xx
        away = pltpu.make_async_remote_copy(
            sbuf.at[q, there], rbuf.at[c, q, mine], xy_send.at[q, off], xy_recv.at[c, q],
            device_id=(chip(yy, z, xx), parity), device_id_type=MESH,
        )
        stays = (off == 0) & (parity == c)

        @pl.when(jnp.logical_not(stays))
        def _():
            if do == "start":
                away.start()
            else:
                away.wait_send()

        if do == "start":
            @pl.when(stays)
            def _():
                pltpu.make_async_copy(sbuf.at[q, there], rbuf.at[c, q, mine], xy_recv.at[c, q]).start()

    def gather_and_send(q):
        rows = xall[q].reshape(g.col, g.dc)
        groups = 4
        per = g.xy // groups
        for i in range(groups):
            got = nn(pick[i * per * g.slots:(i + 1) * per * g.slots, :], rows).astype(BF16)
            sbuf[q, i * per:(i + 1) * per] = got.reshape(per, g.slots, g.dc)

        @pl.loop(0, g.xy)
        def _(off):
            to_plane(q, off, "start")

    for first in range(0, g.nq, 2):
        for step in range(1, g.nz // 2 + 1):
            for q in (first, first + 1):
                for way in range(2):
                    if step <= hops(q, way):
                        z_copy(q, way, step).wait_recv()
                        if step < hops(q, way):
                            z_copy(q, way, step + 1).start()
            if step == g.nz // 2 - 1 and first + 2 < g.nq:
                for q in (first + 2, first + 3):
                    for way in range(2):
                        z_copy(q, way, 1).start()
        for q in (first, first + 1):
            gather_and_send(q)
        if first == 0:
            same = jnp.where(early == late, 1.0, 0.0).astype(BF16)
            pick_t[...] = nt(same, pick[...]).astype(BF16)
            scaled_t[...] = nt(same, scaled[...]).astype(BF16)

    for i in range(3):
        weight_swap(i).wait()

    for q in range(g.nq):
        for kind in range(2):
            pltpu.make_async_copy(rbuf.at[kind, q], rbuf.at[kind, q], xy_recv.at[kind, q]).wait()
        rows = rbuf[0, q].reshape(g.rows, g.dc)
        grads = rbuf[1, q].reshape(g.rows, g.dc)
        feats = slice(q * g.dc, (q + 1) * g.dc)
        if q == 0:
            gacc[...] = nn(rows, wg[feats, :])
            uacc[...] = nn(rows, wu[feats, :])
            hacc[...] = nt(grads, wd[:, feats])
        else:
            gacc[...] += nn(rows, wg[feats, :])
            uacc[...] += nn(rows, wu[feats, :])
            hacc[...] += nt(grads, wd[:, feats])

    for i in range(g.src):
        span = slice(i * g.slots, (i + 1) * g.slots)
        gate_pre, up_pre, grad_hidden = gacc[span, :], uacc[span, :], hacc[span, :]
        sigma = jax.nn.sigmoid(gate_pre)
        down = grad_hidden * (gate_pre * sigma)
        score = jnp.sum(down * up_pre, axis=1, keepdims=True)
        wide = jnp.broadcast_to(score, (g.slots, LANES)).astype(BF16)
        for h in range(2):
            ret0[h, i, :, g.rc:] = wide
        gu[span, :] = down.astype(BF16)
        gg[span, :] = (grad_hidden * up_pre * sigma * (1.0 + gate_pre * (1.0 - sigma))).astype(BF16)

    here_d = y * g.nx + x

    def to_source(j, h, i, do):
        buf, dst = ((ret0, back0), (ret1, back1))[j]
        yy = i // (g.nx // 2)
        xx = 2 * lax.rem(i, g.nx // 2) + lax.rem(c + yy, 2)
        away = pltpu.make_async_remote_copy(
            buf.at[h, i], dst.at[here_d], ret_send.at[j, h, i], ret_recv.at[j],
            device_id=(chip(yy, z, xx), h), device_id_type=MESH,
        )
        stays = (xx == x) & (yy == y) & (c == h)

        @pl.when(jnp.logical_not(stays))
        def _():
            if do == "start":
                away.start()
            else:
                away.wait_send()

        if do == "start":
            @pl.when(stays)
            def _():
                pltpu.make_async_copy(buf.at[h, i], dst.at[here_d], ret_recv.at[j]).start()

    for j in range(2):
        buf = (ret0, ret1)[j]
        for h in range(2):
            feats = slice(h * g.dh + j * g.rc, h * g.dh + (j + 1) * g.rc)
            got = nt(gg[...], wg[feats, :]) + nt(gu[...], wu[feats, :])
            buf[h, :, :, :g.rc] = got.astype(BF16).reshape(g.src, g.slots, g.rc)
        for h in range(2):
            @pl.loop(0, g.src)
            def _(i):
                to_source(j, h, i, "start")

    def combine(j):
        dst = (back0, back1)[j]
        pltpu.make_async_copy(dst, dst, ret_recv.at[j]).wait()
        if j == 0:
            part0[:, :g.rc] = nn(scaled_t[...], back0[:, :, :g.rc].reshape(g.all_slots, g.rc))
            d = lax.broadcasted_iota(jnp.int32, (g.xy, g.slots, LANES), 0)
            at = lax.broadcasted_iota(jnp.int32, (g.xy, g.slots, LANES), 2)
            spot = ((d // g.nx) * g.nz + z) * g.nx + lax.rem(d, g.nx)
            score = jnp.where(at == spot, back0[:, :, g.rc:].astype(F32), 0.0).astype(BF16)
            part0[:, g.rc:] = nn(pick_t[...], score.reshape(g.all_slots, LANES))
        else:
            part1[...] = nn(scaled_t[...], back1[...].reshape(g.all_slots, g.rc))

    def own_part(j, block):
        part = (part0, part1)[j]
        return part[pl.ds(pl.multiple_of(block * g.tok, g.tok), g.tok), :]

    def rs_copy(j, way, step):
        sign = 1 - 2 * way
        src, dst = ((rsend0, rrecv0), (rsend1, rrecv1))[j]
        return pltpu.make_async_remote_copy(
            src.at[way, step - 1], dst.at[way, step - 1], rs_send.at[j, way, step - 1], rs_recv.at[j, way, step - 1],
            device_id=(chip(y, zmod(z + sign), x), c), device_id_type=MESH,
        )

    def rs_step(j, step):
        src, dst = ((rsend0, rrecv0), (rsend1, rrecv1))[j]
        for way in range(2):
            n = hops(j, way)
            if step > n:
                continue
            sign = 1 - 2 * way
            term = own_part(j, zmod(z + sign * (n + 1 - step)))
            if step > 1:
                rs_copy(j, way, step - 1).wait_recv()
                term = term + dst[way, step - 2].astype(F32)
            src[way, step - 1] = term.astype(BF16)
            rs_copy(j, way, step).start()

    def rs_last(j):
        dst = (rrecv0, rrecv1)[j]
        total = own_part(j, z)
        for way in range(2):
            n = hops(j, way)
            rs_copy(j, way, n).wait_recv()
            total = total + dst[way, n - 1].astype(F32)
        return total

    most = g.nz // 2
    combine(0)
    for step in range(1, most):
        rs_step(0, step)
    combine(1)
    rs_step(0, most)
    for step in range(1, most + 1):
        rs_step(1, step)
    first = rs_last(0)
    out_ref[c, :, :g.rc] = first[:, :g.rc].astype(BF16)
    scores = first[:, g.rc:]
    expert_at = lax.broadcasted_iota(jnp.int32, (g.tok, LANES), 1)
    gates = jnp.zeros((g.tok, LANES), F32)
    for k in range(g.top):
        one = jnp.sum(jnp.where(expert_at == ids_ref[:, k:k + 1], scores, 0.0), axis=1, keepdims=True)
        gates = jnp.where(expert_at == k, one, gates)
    gate_ref[...] = gates.astype(BF16)
    out_ref[c, :, g.rc:] = rs_last(1).astype(BF16)

    swap = pltpu.make_async_remote_copy(
        out_ref.at[c], out_ref.at[c], out_send, out_recv, device_id=(e, other), device_id_type=MESH
    )
    swap.start()

    for dz in range(1, g.nz):
        raw_copy(dz).wait_send()
    for q in range(g.nq):
        for way in range(2):
            for step in range(1, hops(q, way) + 1):
                z_copy(q, way, step).wait_send()

        @pl.loop(0, g.xy)
        def _(off):
            to_plane(q, off, "wait")
    for j in range(2):
        for h in range(2):
            @pl.loop(0, g.src)
            def _(i):
                to_source(j, h, i, "wait")
        for way in range(2):
            for step in range(1, hops(j, way) + 1):
                rs_copy(j, way, step).wait_send()
    swap.wait()


def scratch(g):
    dma = pltpu.SemaphoreType.DMA
    half = g.nz // 2
    vm = pltpu.VMEM
    return [
        vm((g.nq, g.nz, g.tok, g.dc), BF16),
        vm((g.nz, 16, LANES), F32),
        vm((g.all_slots, g.col), BF16),
        vm((g.all_slots, g.col), BF16),
        vm((g.col, g.all_slots), BF16),
        vm((g.col, g.all_slots), BF16),
        vm((g.nq, g.xy, g.slots, g.dc), BF16),
        vm((2, g.nq, g.src, g.slots, g.dc), BF16),
        vm((g.dim, g.ff), BF16),
        vm((g.dim, g.ff), BF16),
        vm((g.ff, g.dim), BF16),
        vm((g.rows, g.ff), F32),
        vm((g.rows, g.ff), F32),
        vm((g.rows, g.ff), F32),
        vm((g.rows, g.ff), BF16),
        vm((g.rows, g.ff), BF16),
        vm((2, g.src, g.slots, g.rc + LANES), BF16),
        vm((2, g.src, g.slots, g.rc), BF16),
        vm((g.xy, g.slots, g.rc + LANES), BF16),
        vm((g.xy, g.slots, g.rc), BF16),
        vm((g.col, g.rc + LANES), F32),
        vm((g.col, g.rc), F32),
        vm((2, half, g.tok, g.rc + LANES), BF16),
        vm((2, half, g.tok, g.rc), BF16),
        vm((2, half, g.tok, g.rc + LANES), BF16),
        vm((2, half, g.tok, g.rc), BF16),
        dma((g.nq,)),
        dma((3,)),
        dma((3,)),
        dma((3,)),
        dma((g.nz - 1,)),
        dma((g.nz - 1,)),
        dma((g.nq, 2, half)),
        dma((g.nq, 2, half)),
        dma((g.nq, g.xy)),
        dma((2, g.nq)),
        dma((2, 2, g.src)),
        dma((2,)),
        dma((2, 2, half)),
        dma((2, 2, half)),
        dma(()),
        dma(()),
    ]


def per_device(ny, nz, nx, chunks, tokens, cotangent, expert_ids, gate_weights, w_gate, w_up, w_down):
    tok, dim = tokens.shape
    top = expert_ids.shape[1]
    g = Sizes(tok, dim, w_gate.shape[2], top, ny, nz, nx, chunks)
    z = lax.rem(lax.axis_index("expert") // nx, nz)
    table = jnp.concatenate(
        [
            jnp.pad(expert_ids.astype(F32), ((0, 0), (0, 8 - top)), constant_values=-1.0),
            jnp.pad(gate_weights, ((0, 0), (0, 8 - top))),
        ],
        axis=1,
    ).T
    raw = jnp.where(
        lax.broadcasted_iota(jnp.int32, (16, 2 * tok), 1) // tok == z % 2, jnp.tile(table, (1, 2)), -1.0
    )
    vmem = pl.BlockSpec(memory_space=pltpu.VMEM)
    hbm = pl.BlockSpec(memory_space=pl.ANY)
    halves, gates = pl.pallas_call(
        functools.partial(kernel, g),
        out_shape=(
            jax.ShapeDtypeStruct((2, tok, g.dh), BF16),
            jax.ShapeDtypeStruct((tok, LANES), BF16),
        ),
        in_specs=[vmem, vmem, hbm, hbm, hbm, hbm, hbm],
        out_specs=(vmem, vmem),
        scratch_shapes=scratch(g),
        compiler_params=pltpu.CompilerParams(
            collective_id=0, has_side_effects=True, vmem_limit_bytes=60 * 1024 * 1024
        ),
    )(raw, expert_ids, tokens, cotangent, w_gate, w_up, w_down)
    return jnp.concatenate([halves[0], halves[1]], axis=1), gates[:, :top]


def solution(mesh, ny=NY, nz=NZ, nx=NX, chunks=4):
    placed = (
        P("expert", None),
        P("expert", None),
        P("expert", None),
        P("expert", None),
        P("expert", None, "half"),
        P("expert", None, "half"),
        P("expert", "half", None),
    )
    return jax.shard_map(
        functools.partial(per_device, ny, nz, nx, chunks),
        mesh=mesh,
        in_specs=placed,
        out_specs=(P("expert", None), P("expert", None)),
        check_vma=False,
    )
```

time: 453 us -> 127 us (0.28)
  the two profiles are of different devices: /device:TPU:1 before, /device:TPU:5 now
where the time goes in v1:
time: 127 us; the launch traced here: 126 us
  Pallas kernels  119 us (94%)
  local copies, waits for them, and re-layouts  3.82 us (3%)
  other arithmetic  2.71 us (2%)
    pallas_call x1, Pallas kernels, per_device(): pl.pallas_call(functools.partial(kernel, g), out_shape=(jax.ShapeDtypeStr...  119 us
    unnamed x2, local copies, waits for them, and re-layouts  2.75 us

profile of v1, /device:TPU:5, one launch (start us, length us, event | category | flops | bytes accessed | tf_op | source)
XLA Modules:
  0.0 126.3 jit_solution(9936407746046606067)
XLA Ops:
  0.7 0.7 convert_element_type.3
  1.4 0.7 maximum_bitcast_fusion
  2.1 0.1 tile.10
  2.2 0.6 fusion.raw_ref
  2.8 1.4 %copy.9.ids_ref = s32[64,8]{1,0:T(8,128)} copy(s32[64,8]{0,1:T(8,128)} %param.9) | data formatting | bytes 4096 | tf_op args[2]
  4.1 119.0 %shard_map.86 = (bf16[2,64,1024]{2,1,0:T(8,128)(2,1)}, bf16[64,128]{1,0:T(8,128)(2,1)}) custom-call(f32[16,128]{1,0:T(8,128)} %fusion.raw_ref, s32[64,8]{1,0:T(8,128)} %copy.9.ids_ref, bf16[64,2048]{1,0:T(8,128)(2,1)} %tok_hbm.1, bf16[64,2048]{1,0:T(8,128)(2,1)} %cot_hbm.1, bf16[1,2048,384]{2,1,0:T(8,128)(2,1)} %wg_hbm.1, bf16[1,2048,384]{2,1,0:T(8,128)(2,1)} %wu_hbm.1, ...), custom_call_target="tpu_custom_call" | custom-call | tf_op jit(solution)/shard_map/pallas_call | solution.py:437
  123.2 1.4 %copy.10 = bf16[64,8]{0,1:T(8,128)(2,1)} copy(bf16[64,8]{1,0:T(8,128)(2,1)} %bitcast.7) | data formatting | bytes 2048
  124.5 1.0 slice_bitcast_fusion.1
  125.5 0.7 pad_maximum_fusion
  (3 shorter events, 0.0 us)

commit v2 on v0

v2 whole, which is shorter than its diff:
```python
import functools

import jax
import jax.numpy as jnp
from jax import lax
from jax.experimental import pallas as pl
from jax.experimental.pallas import tpu as pltpu
from jax.sharding import PartitionSpec as P

MESH = pl.DeviceIdType.MESH
F32 = jnp.float32
BF16 = jnp.bfloat16
NY, NZ, NX = 4, 8, 4
CAP = 6
LANES = 128


def nt(a, b):
    return lax.dot_general(a, b, (((1,), (1,)), ((), ())), preferred_element_type=F32)


def nn(a, b):
    return jnp.dot(a, b, preferred_element_type=F32)


class Sizes:
    def __init__(self, tok, dim, half_ff, top, ny, nz, nx, ahead, widths):
        self.tok, self.dim, self.hf, self.ff, self.top = tok, dim, half_ff, 2 * half_ff, top
        self.ny, self.nz, self.nx = ny, nz, nx
        self.ahead = ahead
        self.starts = [sum(ahead[:q]) for q in range(len(ahead))]
        self.nq = len(ahead)
        self.xy = ny * nx
        self.src = self.xy // 2
        self.slots = CAP * nz
        self.rows = self.src * self.slots
        self.all_slots = self.xy * self.slots
        self.col = nz * tok
        self.dh = dim // 2
        self.widths = widths
        self.cuts = [sum(widths[1:j]) for j in range(len(widths))]
        self.nj = len(widths)
        self.direct = self.nj - 1


def hops_of(number, way, half):
    return half if (number + way) % 2 == 0 else half - 1


def ring_plan(widths, half):
    lag, per_lane, fill = 2.1, 0.00275, 0.8
    link, now, waiting, plan = [0.0, 0.0], 0.0, [], []
    left = [2 * half - 1] * len(widths)
    fresh, tables = 0, False

    def send(q, way, step):
        link[way] = max(link[way], now) + per_lane * widths[q]
        waiting.append((link[way] + lag, q, way, step))

    while fresh < len(widths) or waiting:
        soonest = min(waiting)[0] if waiting else now
        if fresh < len(widths) and max(max(link), now) <= soonest:
            plan.append(("first", fresh))
            for way in range(2):
                send(fresh, way, 1)
            fresh += 1
            continue
        at, q, way, step = min(waiting)
        waiting.remove((at, q, way, step))
        now = max(now, at)
        if now > 4.4 and not tables:
            tables = True
            plan.append(("tables",))
        plan.append(("wait", q, way, step))
        if step < hops_of(q, way, half):
            send(q, way, step + 1)
        left[q] -= 1
        if not left[q]:
            plan.append(("gather", q))
            now += fill
    return plan


def sum_plan(widths, half, direct):
    now, plane, link = 0.0, 0.0, 0.0
    ready, made, plan = [], 0, []
    while made < len(widths) or ready:
        due = made < len(widths) and plane - now < 2.5
        soonest = min(ready) if ready else None
        if made < len(widths) and (due or soonest is None or soonest[0] > now):
            w = widths[made]
            plan.append(("make", made))
            now += 0.5 if made == 0 else 0.0078 * w
            plane = max(plane, now) + 0.0168 * w
            ready.append((plane + 1.5, made, 0))
            made += 1
            continue
        at, j, step = soonest
        ready.remove(soonest)
        now = max(now, at)
        w = widths[j]
        if step == 0:
            plan.append(("combine", j))
            now += 0.3 + 0.001 * w
        last = 1 if j == direct else half
        if step == last:
            plan.append(("last", j))
            now += 0.3
            continue
        if step:
            plan.append(("add", j, step + 1))
            now += 0.3
        link = max(link, now) + (0.022 if j == direct else 0.00275) * w
        ready.append((link + (4.0 if j == direct else 2.1), j, step + 1))
    return plan


def kernel(
    g, ids_hbm, gates_hbm, tok_hbm, cot_hbm, wg_hbm, wu_hbm, wd_hbm, out_ref, gate_ref,
    ids_ref, gates_ref, xall, rawall, pick, scaled, pick_t, scaled_t, sbuf, rbuf, wg, wu, wd, gacc, uacc, hacc, gg, gu,
    table_sem, own_sem, w_own_sem, w_send, w_recv, raw_send, raw_recv, z_send, z_recv, xy_send, xy_recv,
    ret_send, ret_recv, rs_send, rs_recv, out_send, out_recv, *lists,
):
    ret, back, part, rsend, rrecv = (lists[k * g.nj:(k + 1) * g.nj] for k in range(5))
    e = lax.axis_index("expert")
    c = lax.axis_index("half")
    x = lax.rem(e, g.nx)
    z = lax.rem(e // g.nx, g.nz)
    y = e // (g.nx * g.nz)
    other = 1 - c
    parity = lax.rem(x + y, 2)

    def chip(yy, zz, xx):
        return (yy * g.nz + zz) * g.nx + xx

    def zmod(v):
        return lax.rem(v + 2 * g.nz, g.nz)

    tables_in = (
        pltpu.make_async_copy(ids_hbm, ids_ref, table_sem.at[0]),
        pltpu.make_async_copy(gates_hbm, gates_ref, table_sem.at[1]),
    )
    for copy in tables_in:
        copy.start()

    @pl.when(c == 0)
    def _():
        pltpu.make_async_copy(tok_hbm, xall.at[z], own_sem).start()

    @pl.when(c == 1)
    def _():
        pltpu.make_async_copy(cot_hbm, xall.at[z], own_sem).start()

    cut = pl.ds(pl.multiple_of(c * g.hf, LANES), g.hf)
    places = (wg.at[:, cut], wu.at[:, cut], wd.at[cut, :])
    weights = (wg_hbm.at[0], wu_hbm.at[0], wd_hbm.at[0])

    def weight_own(i):
        return pltpu.make_async_copy(weights[i], places[i], w_own_sem.at[i])

    def weight_swap(i):
        return pltpu.make_async_remote_copy(
            places[i], places[i], w_send.at[i], w_recv.at[i], device_id=(e, other), device_id_type=MESH
        )

    barrier = pltpu.get_barrier_semaphore()
    for dz in range(1, g.nz):
        pl.semaphore_signal(barrier, inc=1, device_id=(chip(y, zmod(z + dz), x), c), device_id_type=MESH)
    for dy in range(g.ny):
        for dx in range(g.nx):
            peer = chip(lax.rem(y + dy, g.ny), z, lax.rem(x + dx, g.nx))
            if dy or dx:
                pl.semaphore_signal(barrier, inc=1, device_id=(peer, c), device_id_type=MESH)
            pl.semaphore_signal(barrier, inc=1, device_id=(peer, other), device_id_type=MESH)
    for i in range(3):
        weight_own(i).start()
    for copy in tables_in:
        copy.wait()
    table = jnp.concatenate([ids_ref[...].astype(F32), gates_ref[...]], axis=0)
    rawall[z] = jnp.concatenate([table, table], axis=1)
    pl.semaphore_wait(barrier, 2 * g.xy - 1 + g.nz - 1)

    def raw_copy(dz):
        return pltpu.make_async_remote_copy(
            rawall.at[z], rawall.at[z], raw_send, raw_recv,
            device_id=(chip(y, zmod(z + dz), x), c), device_id_type=MESH,
        )

    for dz in range(1, g.nz):
        raw_copy(dz).start()

    def hops(number, way):
        return hops_of(number, way, g.nz // 2)

    def lanes(q):
        return pl.ds(g.starts[q], g.ahead[q])

    def z_copy(q, way, step):
        sign = 1 - 2 * way
        rows = xall.at[zmod(z - sign * (step - 1)), :, lanes(q)]
        return pltpu.make_async_remote_copy(
            rows, rows, z_send, z_recv.at[q, way, step - 1],
            device_id=(chip(y, zmod(z + sign), x), c), device_id_type=MESH,
        )

    pltpu.make_async_copy(tok_hbm, xall.at[z], own_sem).wait()

    def tables():
        pltpu.make_async_copy(rawall.at[pl.ds(0, g.nz - 1)], rawall.at[pl.ds(0, g.nz - 1)], raw_recv).wait()
        lane = lax.broadcasted_iota(jnp.int32, (2 * g.top, LANES), 1)
        pairs = [
            jnp.where(lane < g.tok, rawall[2 * p], rawall[2 * p + 1]) for p in range(g.nz // 2)
        ]
        raw = jnp.concatenate(pairs, axis=1)
        place = lax.broadcasted_iota(jnp.int32, (g.xy, g.col), 0)
        named_by = (((place // g.nx) * g.nz + z) * g.nx + lax.rem(place, g.nx)).astype(F32)
        named = jnp.zeros((g.xy, g.col), F32)
        weight = jnp.zeros((g.xy, g.col), F32)
        for k in range(g.top):
            hit = raw[k:k + 1, :] == named_by
            named = named + jnp.where(hit, 1.0, 0.0)
            weight = weight + jnp.where(hit, raw[g.top + k:g.top + k + 1, :], 0.0)
        early = lax.broadcasted_iota(jnp.int32, (g.col, g.col), 0)
        late = lax.broadcasted_iota(jnp.int32, (g.col, g.col), 1)
        before = jnp.where((early // g.tok == late // g.tok) & (early < late), 1.0, 0.0).astype(BF16)
        rank = nn(named.astype(BF16), before)
        token = lax.broadcasted_iota(jnp.int32, (g.xy, g.col), 1)
        key = jnp.where(named > 0.0, rank + (CAP * (token // g.tok)).astype(F32), -1.0)
        slot = lax.broadcasted_iota(jnp.int32, (g.slots, g.col), 0).astype(F32)
        for d in range(g.xy):
            hit = key[d:d + 1, :] == slot
            pick[d * g.slots:(d + 1) * g.slots, :] = jnp.where(hit, 1.0, 0.0).astype(BF16)
            scaled[d * g.slots:(d + 1) * g.slots, :] = jnp.where(hit, weight[d:d + 1, :], 0.0).astype(BF16)

    mine = y * (g.nx // 2) + x // 2

    def to_plane(q, off):
        yy = lax.rem(y + off // g.nx, g.ny)
        xx = lax.rem(x + lax.rem(off, g.nx), g.nx)
        src = sbuf.at[yy * g.nx + xx, :, lanes(q)]
        dst = rbuf.at[c, mine, :, lanes(q)]
        stays = (off == 0) & (parity == c)

        @pl.when(jnp.logical_not(stays))
        def _():
            pltpu.make_async_remote_copy(
                src, dst, xy_send, xy_recv.at[c, q], device_id=(chip(yy, z, xx), parity), device_id_type=MESH
            ).start()

        @pl.when(stays)
        def _():
            pltpu.make_async_copy(src, dst, xy_recv.at[c, q]).start()

    def gather_and_send(q):
        rows = xall[:, :, g.starts[q]:g.starts[q] + g.ahead[q]].reshape(g.col, g.ahead[q])
        groups = 4
        per = g.xy // groups
        for i in range(groups):
            got = nn(pick[i * per * g.slots:(i + 1) * per * g.slots, :], rows).astype(BF16)
            sbuf[i * per:(i + 1) * per, :, g.starts[q]:g.starts[q] + g.ahead[q]] = got.reshape(per, g.slots, g.ahead[q])

        @pl.loop(0, g.xy)
        def _(off):
            to_plane(q, off)

    swapped = False
    for step in ring_plan(g.ahead, g.nz // 2):
        if step[0] == "first":
            for way in range(2):
                z_copy(step[1], way, 1).start()
        elif step[0] == "tables":
            tables()
        elif step[0] == "wait":
            _, q, way, at = step
            z_copy(q, way, at).wait_recv()
            if at < hops(q, way):
                z_copy(q, way, at + 1).start()
        else:
            gather_and_send(step[1])
            if not swapped:
                swapped = True
                for i in range(3):
                    weight_own(i).wait()
                    weight_swap(i).start()

    early = lax.broadcasted_iota(jnp.int32, (g.col, g.col), 0)
    late = lax.broadcasted_iota(jnp.int32, (g.col, g.col), 1)
    same = jnp.where(early == late, 1.0, 0.0).astype(BF16)
    pick_t[...] = nt(same, pick[...]).astype(BF16)
    scaled_t[...] = nt(same, scaled[...]).astype(BF16)

    for i in range(3):
        weight_swap(i).wait()

    for q in range(g.nq):
        feats = slice(g.starts[q], g.starts[q] + g.ahead[q])
        for kind in range(2):
            came = rbuf.at[kind, :, :, lanes(q)]
            pltpu.make_async_copy(came, came, xy_recv.at[kind, q]).wait()
        rows = rbuf[0, :, :, feats].reshape(g.rows, g.ahead[q])
        grads = rbuf[1, :, :, feats].reshape(g.rows, g.ahead[q])
        if q == 0:
            gacc[...] = nn(rows, wg[feats, :])
            uacc[...] = nn(rows, wu[feats, :])
            hacc[...] = nt(grads, wd[:, feats])
        else:
            gacc[...] += nn(rows, wg[feats, :])
            uacc[...] += nn(rows, wu[feats, :])
            hacc[...] += nt(grads, wd[:, feats])

    for i in range(g.src):
        span = slice(i * g.slots, (i + 1) * g.slots)
        gate_pre, up_pre, grad_hidden = gacc[span, :], uacc[span, :], hacc[span, :]
        sigma = jax.nn.sigmoid(gate_pre)
        down = grad_hidden * (gate_pre * sigma)
        score = jnp.sum(down * up_pre, axis=1, keepdims=True)
        wide = jnp.broadcast_to(score, (g.slots, LANES)).astype(BF16)
        ret[0][0, i] = wide
        gu[span, :] = down.astype(BF16)
        gg[span, :] = (grad_hidden * up_pre * sigma * (1.0 + gate_pre * (1.0 - sigma))).astype(BF16)

    here_d = y * g.nx + x

    def to_source(j, h, i):
        src = ret[j].at[h if j else 0, i]
        dst = back[j].at[here_d]
        yy = i // (g.nx // 2)
        xx = 2 * lax.rem(i, g.nx // 2) + lax.rem(c + yy, 2)
        stays = (xx == x) & (yy == y) & (c == h)

        @pl.when(jnp.logical_not(stays))
        def _():
            pltpu.make_async_remote_copy(
                src, dst, ret_send.at[j], ret_recv.at[j], device_id=(chip(yy, z, xx), h), device_id_type=MESH
            ).start()

        @pl.when(stays)
        def _():
            pltpu.make_async_copy(src, dst, ret_recv.at[j]).start()

    def make(j):
        for h in range(2):
            if j:
                feats = slice(h * g.dh + g.cuts[j], h * g.dh + g.cuts[j] + g.widths[j])
                got = nt(gg[...], wg[feats, :]) + nt(gu[...], wu[feats, :])
                ret[j][h] = got.astype(BF16).reshape(g.src, g.slots, g.widths[j])

            @pl.loop(0, g.src)
            def _(i):
                to_source(j, h, i)

    def combine(j):
        pltpu.make_async_copy(back[j], back[j], ret_recv.at[j]).wait()
        if j == 0:
            d = lax.broadcasted_iota(jnp.int32, (g.xy, g.slots, LANES), 0)
            at = lax.broadcasted_iota(jnp.int32, (g.xy, g.slots, LANES), 2)
            spot = ((d // g.nx) * g.nz + z) * g.nx + lax.rem(d, g.nx)
            score = jnp.where(at == spot, back[0][...].astype(F32), 0.0).astype(BF16)
            part[0][...] = nn(pick_t[...], score.reshape(g.all_slots, LANES))
        else:
            part[j][...] = nn(scaled_t[...], back[j][...].reshape(g.all_slots, g.widths[j]))

    def own_part(j, block):
        return part[j][pl.ds(pl.multiple_of(block * g.tok, g.tok), g.tok), :]

    def spot(j, way, step):
        return step - 1 + way * hops(j, 0)

    def rs_copy(j, way, step):
        sign = 1 - 2 * way
        n = spot(j, way, step)
        return pltpu.make_async_remote_copy(
            rsend[j].at[n], rrecv[j].at[n], rs_send.at[j], rs_recv.at[j, n],
            device_id=(chip(y, zmod(z + sign), x), c), device_id_type=MESH,
        )

    def rs_step(j, step):
        for way in range(2):
            n = hops(j, way)
            if step > n:
                continue
            sign = 1 - 2 * way
            term = own_part(j, zmod(z + sign * (n + 1 - step)))
            if step > 1:
                rs_copy(j, way, step - 1).wait_recv()
                term = term + rrecv[j][spot(j, way, step - 1)].astype(F32)
            rsend[j][spot(j, way, step)] = term.astype(BF16)
            rs_copy(j, way, step).start()

    def rs_direct(j):
        for dz in sorted(range(1, g.nz), key=lambda v: -min(v, g.nz - v)):
            there = zmod(z + dz)
            rsend[j][dz - 1] = own_part(j, there).astype(BF16)
            pltpu.make_async_remote_copy(
                rsend[j].at[dz - 1], rrecv[j].at[dz - 1], rs_send.at[j], rs_recv.at[j, 0],
                device_id=(chip(y, there, x), c), device_id_type=MESH,
            ).start()

    def swap(j):
        span = pl.ds(pl.multiple_of(c * g.dh + g.cuts[j], LANES), g.widths[j])
        return pltpu.make_async_remote_copy(
            out_ref.at[:, span], out_ref.at[:, span], out_send, out_recv,
            device_id=(e, other), device_id_type=MESH,
        )

    def rs_last(j):
        total = own_part(j, z)
        if j == g.direct:
            pltpu.make_async_copy(rrecv[j], rrecv[j], rs_recv.at[j, 0]).wait()
            for n in range(g.nz - 1):
                total = total + rrecv[j][n].astype(F32)
        else:
            for way in range(2):
                rs_copy(j, way, hops(j, way)).wait_recv()
                total = total + rrecv[j][spot(j, way, hops(j, way))].astype(F32)
        if j:
            out_ref[:, pl.ds(pl.multiple_of(c * g.dh + g.cuts[j], LANES), g.widths[j])] = total.astype(BF16)
            swap(j).start()
        else:
            square = (LANES, LANES)
            same = lax.broadcasted_iota(jnp.int32, square, 0) == lax.broadcasted_iota(jnp.int32, square, 1)
            scores = nt(jnp.where(same, 1.0, 0.0).astype(BF16), total.astype(BF16))
            expert_at = lax.broadcasted_iota(jnp.int32, (LANES, g.tok), 0)
            for k in range(g.top):
                one = jnp.where(expert_at == ids_ref[k:k + 1, :], scores, 0.0)
                gate_ref[k:k + 1, :] = jnp.sum(one, axis=0, keepdims=True)

    for step in sum_plan(g.widths, g.nz // 2, g.direct):
        if step[0] == "make":
            make(step[1])
        elif step[0] == "combine":
            combine(step[1])
            if step[1] == g.direct:
                rs_direct(step[1])
            else:
                rs_step(step[1], 1)
        elif step[0] == "add":
            rs_step(step[1], step[2])
        else:
            rs_last(step[1])

    def gone(ref, sem):
        pltpu.make_async_copy(ref, ref, sem).wait()

    some = pl.ds(0, g.nz - 1)
    gone(rawall.at[some], raw_send)
    gone(xall.at[some], z_send)
    for j in range(g.nj):
        gone(rsend[j], rs_send.at[j])

    @pl.when(parity == c)
    def _():
        fewer = pl.ds(0, g.xy - 1)
        gone(sbuf.at[fewer], xy_send)
        for j in range(g.nj):
            gone(back[j].at[fewer], ret_send.at[j])

    @pl.when(parity != c)
    def _():
        gone(sbuf, xy_send)
        for j in range(g.nj):
            gone(back[j], ret_send.at[j])

    half = out_ref.at[:, pl.ds(0, g.dh)]
    gone(half, out_send)
    gone(half, out_recv)


def scratch(g):
    dma = pltpu.SemaphoreType.DMA
    half = g.nz // 2
    vm = pltpu.VMEM
    return [
        vm((g.top, g.tok), jnp.int32),
        vm((g.top, g.tok), F32),
        vm((g.nz, g.tok, g.dim), BF16),
        vm((g.nz, 2 * g.top, LANES), F32),
        vm((g.all_slots, g.col), BF16),
        vm((g.all_slots, g.col), BF16),
        vm((g.col, g.all_slots), BF16),
        vm((g.col, g.all_slots), BF16),
        vm((g.xy, g.slots, g.dim), BF16),
        vm((2, g.src, g.slots, g.dim), BF16),
        vm((g.dim, g.ff), BF16),
        vm((g.dim, g.ff), BF16),
        vm((g.ff, g.dim), BF16),
        vm((g.rows, g.ff), F32),
        vm((g.rows, g.ff), F32),
        vm((g.rows, g.ff), F32),
        vm((g.rows, g.ff), BF16),
        vm((g.rows, g.ff), BF16),
        dma((2,)),
        dma(()),
        dma((3,)),
        dma((3,)),
        dma((3,)),
        dma(()),
        dma(()),
        dma(()),
        dma((g.nq, 2, half)),
        dma(()),
        dma((2, g.nq)),
        dma((g.nj,)),
        dma((g.nj,)),
        dma((g.nj,)),
        dma((g.nj, g.nz - 1)),
        dma(()),
        dma(()),
        *[vm((2 if j else 1, g.src, g.slots, w), BF16) for j, w in enumerate(g.widths)],
        *[vm((g.xy, g.slots, w), BF16) for w in g.widths],
        *[vm((g.col, w), F32) for w in g.widths],
        *[vm((g.nz - 1, g.tok, w), BF16) for w in g.widths],
        *[vm((g.nz - 1, g.tok, w), BF16) for w in g.widths],
    ]


def per_device(ny, nz, nx, ahead, widths, tokens, cotangent, expert_ids, gate_weights, w_gate, w_up, w_down):
    tok, dim = tokens.shape
    top = expert_ids.shape[1]
    g = Sizes(tok, dim, w_gate.shape[2], top, ny, nz, nx, ahead, widths)
    vmem = pl.BlockSpec(memory_space=pltpu.VMEM)
    hbm = pl.BlockSpec(memory_space=pl.ANY)
    input_grad, gate_grad = pl.pallas_call(
        functools.partial(kernel, g),
        out_shape=(
            jax.ShapeDtypeStruct((tok, dim), BF16),
            jax.ShapeDtypeStruct((top, tok), F32),
        ),
        in_specs=[hbm] * 7,
        out_specs=(vmem, vmem),
        scratch_shapes=scratch(g),
        compiler_params=pltpu.CompilerParams(
            collective_id=0, has_side_effects=True, vmem_limit_bytes=60 * 1024 * 1024
        ),
    )(expert_ids.T, gate_weights.T, tokens, cotangent, w_gate, w_up, w_down)
    return input_grad, gate_grad.T.astype(BF16)


def solution(mesh, ny=NY, nz=NZ, nx=NX, ahead=(128, 128) + (256,) * 7, widths=(LANES, 128, 256, 256, 256, 128)):
    placed = (
        P("expert", None),
        P("expert", None),
        P("expert", None),
        P("expert", None),
        P("expert", None, "half"),
        P("expert", None, "half"),
        P("expert", "half", None),
    )
    return jax.shard_map(
        functools.partial(per_device, ny, nz, nx, ahead, widths),
        mesh=mesh,
        in_specs=placed,
        out_specs=(P("expert", None), P("expert", None)),
        check_vma=False,
    )
```

time: 453 us -> 106 us (0.23)
  waiting for transfers between devices: 198 us -> 0 us
  blocking collectives: 112 us -> 0 us
  Pallas kernels: 0 us -> 101 us
  local copies, waits for them, and re-layouts: 50.7 us -> 1.67 us
  starting transfers between devices: 36.7 us -> 0 us
  matrix products: 27.6 us -> 0 us
  between operations: 14.2 us -> 0.64 us
  other arithmetic: 10.1 us -> 1.26 us
    all_to_all x3 -> x0, waiting for transfers between devices: 177 us -> none  [the longest x1 88.1 us: per_device(): lax.all_to_all(input_full, 'expert', split_axis=0, concat_axis=0, tiled=T...]
    all_to_all x1 -> x0, blocking collectives: 110 us -> none  [per_device(): lax.all_to_all(sent_grads, 'expert', split_axis=0, concat_axis=0, tiled=T...]
    pallas_call x0 -> x1, Pallas kernels: none -> 101 us  [per_device(): pl.pallas_call(functools.partial(kernel, g), out_shape=(jax.ShapeDtypeStr...]
    all_to_all x3 -> x0, starting transfers between devices: 36.5 us -> none  [the longest x1 13.6 us: per_device(): lax.all_to_all(scores, 'expert', split_axis=0, concat_axis=0, tiled=True)]
    gather x6 -> x0, local copies, waits for them, and re-layouts: 32.3 us -> none  [the longest x2 10.6 us: per_device(): cotangent[picked]]
    dot_general x6 -> x0, matrix products: 27.6 us -> none  [the longest x1 6.29 us: expert_terms(): jnp.einsum('ncd,fd->ncf', grads, down_one, preferred_element_type=jnp.flo...]
    reduce_scatter x1 -> x0, waiting for transfers between devices: 18.8 us -> none  [per_device(): lax.psum_scatter(input_part, 'half', scatter_dimension=2, tiled=True)]
    reshape x3 -> x0, local copies, waits for them, and re-layouts: 6.57 us -> none  [the longest x1 6.33 us: owner_sum(): picked = back.reshape(-1, width)[slot_index]]
  transfers between devices with their start and end apart: 5 -> 0, of which waited for: 5 -> 0; matrix products, arithmetic and copies ran while one was open for 4% -> 0% of each run, Pallas kernels for 0% -> 0%
where the time goes in v2:
time: 106 us; the launch traced here: 105 us
  Pallas kernels  101 us (95%)
  local copies, waits for them, and re-layouts  1.67 us (2%)
  other arithmetic  1.26 us (1%)
    pallas_call x1, Pallas kernels, per_device(): pl.pallas_call(functools.partial(kernel, g), out_shape=(jax.ShapeDtypeStr...  101 us

profile of v2, /device:TPU:1, one launch (start us, length us, event | category | flops | bytes accessed | tf_op | source)
XLA Modules:
  0.0 104.6 jit_solution(14584094348858073467)
XLA Ops:
  0.6 101.0 %shard_map.86 = (bf16[64,2048]{1,0:T(8,128)(2,1)}, f32[8,64]{1,0:T(8,128)}) custom-call(s32[8,64]{1,0:T(8,128)} %bitcast.4, f32[8,64]{1,0:T(8,128)} %bitcast.5, bf16[64,2048]{1,0:T(8,128)(2,1)} %tok_hbm.1, bf16[64,2048]{1,0:T(8,128)(2,1)} %cot_hbm.1, bf16[1,2048,384]{2,1,0:T(8,128)(2,1)} %wg_hbm.1, bf16[1,2048,384]{2,1,0:T(8,128)(2,1)} %wu_hbm.1, ...), custom_call_target="tpu_custom_call" | custom-call | tf_op jit(solution)/shard_map/pallas_call | solution.py:523
  101.6 1.3 %convert_bitcast_fusion = bf16[64,8]{0,1:T(8,128)(2,1)} fusion(f32[8,64]{1,0:T(8,128)} %get-tuple-element.5), kind=kLoop, calls=%fused_computation | loop fusion | flops 512 | bytes 3072 | tf_op jit(solution)/shard_map/convert_element_type | solution.py:536
  102.9 1.7 %copy.10 = bf16[64,2048]{1,0:T(8,128)(2,1)} copy(bf16[64,2048]{1,0:T(8,128)(2,1)} %get-tuple-element.8) | data formatting | bytes 524288

commit v3 on v2

v3 whole, which is shorter than its diff:
```python
import functools

import jax
import jax.numpy as jnp
from jax import lax
from jax.experimental import pallas as pl
from jax.experimental.pallas import tpu as pltpu
from jax.sharding import PartitionSpec as P

MESH = pl.DeviceIdType.MESH
F32 = jnp.float32
BF16 = jnp.bfloat16
NY, NZ, NX = 4, 8, 4
CAP = 6
LANES = 128


def nt(a, b):
    return lax.dot_general(a, b, (((1,), (1,)), ((), ())), preferred_element_type=F32)


def nn(a, b):
    return jnp.dot(a, b, preferred_element_type=F32)


class Sizes:
    def at(self, away):
        return self.order.index(away % self.nz)

    def __init__(self, tok, dim, half_ff, top, ny, nz, nx, ahead, near, widths, direct):
        self.tok, self.dim, self.hf, self.ff, self.top = tok, dim, half_ff, 2 * half_ff, top
        self.ny, self.nz, self.nx = ny, nz, nx
        self.ahead = ahead
        self.starts = [sum(ahead[:q]) for q in range(len(ahead))]
        self.nq = len(ahead)
        self.near = near
        self.order = [0] + [v for k in range(1, nz // 2) for v in (k, nz - k)] + [nz // 2]
        self.early = 16
        self.reach = 3
        self.xy = ny * nx
        self.src = self.xy // 2
        self.slots = CAP * nz
        self.rows = self.src * self.slots
        self.all_slots = self.xy * self.slots
        self.col = nz * tok
        self.dh = dim // 2
        self.widths = widths
        self.cuts = [sum(widths[1:j]) for j in range(len(widths))]
        self.nj = len(widths)
        self.direct = direct


def hops_of(number, way, half):
    return half if (number + way) % 2 == 0 else half - 1


def ring_plan(widths, near, half):
    lag, per_lane, hop = 2.3, 0.0036, 2.9
    size = [0.0]
    for w in widths:
        size.append(size[-1] + w / sum(widths))
    sends, came = [], {}
    for way in range(2):
        ready = {(q, 1): 0.0 for q in range(len(widths))}
        link = 0.0
        while ready:
            def due(item):
                q, step = item
                last = 15.5 + 23.0 * size[q] - hop * (hops_of(q, way, half) - step)
                return min(last, 4.0 + 11.4 * size[q]) if step == 1 else last

            now = max(link, min(ready.values()))
            q, step = min((item for item in ready if ready[item] <= now), key=due)
            del ready[q, step]
            sends.append((now, 0, "send", q, way, step))
            link = now + per_lane * widths[q]
            came[q, way, step] = link + lag
            if step < hops_of(q, way, half):
                ready[q, step + 1] = link + lag
    events = [(4.4, 1, "tables")]
    first = [max(came[q, way, 1] for q in group for way in range(2)) for group in near]
    events += [(max(4.9, t), 2, "near", n) for n, t in enumerate(first)]
    latest = max(4.9, max(first))
    for q in range(len(widths)):
        t = max(v for k, v in came.items() if k[0] == q)
        events.append((max(t, latest + 0.01), 3, "far", q))
    return [event[2:] for event in sorted(sends + events)]


def sum_plan(widths, half, direct, early):
    count = len(widths)
    plan, events, now, plane, link = [], [], 0.0, 0.0, 0.0
    for j in [1, 0, *range(2, count)]:
        plan.append(("make", j))
        now += 1.8 if j else 0.4
        plane = max(plane, now) + (0.0168 * widths[j] * (1.0 - early) if j else 0.7)
        events.append((plane + 3.8, "combine", j, 0))
    close = [0.0] * count
    for j in range(1, count):
        plan.append(("near", j))
        now += 0.4
        plane = max(plane, now) + 0.0168 * widths[j] * early
        close[j] = plane + 3.8
    while events:
        at, kind, j, step = min(events)
        events.remove((at, kind, j, step))
        now = max(now, at)
        plan.append((kind, j, step))
        now += {"combine": 0.5, "add": 0.25, "close": 0.6, "last": 0.3}[kind]
        if kind == "last":
            continue
        if j in direct:
            units = 7.0 if kind == "combine" else 1.0
        else:
            units = 1.0
        link = max(link, now) + 0.0036 * units * widths[j]
        there = link + (4.1 if j in direct and kind == "combine" else 2.3)
        hops = half if j == 0 else half - 1
        if kind == "close" or (j == 0 and step == hops - 1):
            events.append((there, "last", j, 0))
        elif j in direct or step == hops - 1:
            events.append((close[j] if j in direct else max(close[j], there), "close", j, 0))
        else:
            events.append((there, "add", j, step + 1))
    return plan


def kernel(
    g, ids_hbm, gates_hbm, tok_hbm, cot_hbm, wg_hbm, wu_hbm, wd_hbm, out_ref, gate_ref,
    ids_ref, gates_ref, xall, rawall, pick_near, pick_far, pick, scaled, pick_t, near_t, far_t, sbuf, rbuf, wg, wu, wd, gacc, uacc, hacc, gg, gu,
    table_sem, own_sem, w_own_sem, w_send, w_recv, raw_send, raw_recv, z_send, z_recv, xy_send, near_recv, xy_recv,
    ret_send, ret_recv, back_recv, rs_send, rs_recv, out_send, out_recv, *lists,
):
    ret, back, part, rsend, rrecv = (lists[k * g.nj:(k + 1) * g.nj] for k in range(5))
    e = lax.axis_index("expert")
    c = lax.axis_index("half")
    x = lax.rem(e, g.nx)
    z = lax.rem(e // g.nx, g.nz)
    y = e // (g.nx * g.nz)
    other = 1 - c
    parity = lax.rem(x + y, 2)

    def chip(yy, zz, xx):
        return (yy * g.nz + zz) * g.nx + xx

    def zmod(v):
        return lax.rem(v + 2 * g.nz, g.nz)

    tables_in = (
        pltpu.make_async_copy(ids_hbm, ids_ref, table_sem.at[0]),
        pltpu.make_async_copy(gates_hbm, gates_ref, table_sem.at[1]),
    )
    for copy in tables_in:
        copy.start()

    @pl.when(c == 0)
    def _():
        pltpu.make_async_copy(tok_hbm, xall.at[0], own_sem).start()

    @pl.when(c == 1)
    def _():
        pltpu.make_async_copy(cot_hbm, xall.at[0], own_sem).start()

    cut = pl.ds(pl.multiple_of(c * g.hf, LANES), g.hf)
    places = (wg.at[:, cut], wu.at[:, cut], wd.at[cut, :])
    weights = (wg_hbm.at[0], wu_hbm.at[0], wd_hbm.at[0])

    def weight_own(i):
        return pltpu.make_async_copy(weights[i], places[i], w_own_sem.at[i])

    def weight_swap(i):
        return pltpu.make_async_remote_copy(
            places[i], places[i], w_send.at[i], w_recv.at[i], device_id=(e, other), device_id_type=MESH
        )

    barrier = pltpu.get_barrier_semaphore()
    for dz in range(1, g.nz):
        pl.semaphore_signal(barrier, inc=1, device_id=(chip(y, zmod(z + dz), x), c), device_id_type=MESH)
    for dy in range(g.ny):
        for dx in range(g.nx):
            peer = chip(lax.rem(y + dy, g.ny), z, lax.rem(x + dx, g.nx))
            if dy or dx:
                pl.semaphore_signal(barrier, inc=1, device_id=(peer, c), device_id_type=MESH)
            pl.semaphore_signal(barrier, inc=1, device_id=(peer, other), device_id_type=MESH)
    for i in range(3):
        weight_own(i).start()
    for copy in tables_in:
        copy.wait()
    table = jnp.concatenate([ids_ref[...].astype(F32), gates_ref[...]], axis=0)
    rawall[0] = jnp.concatenate([table, table], axis=1)
    pl.semaphore_wait(barrier, 2 * g.xy - 1 + g.nz - 1)

    def raw_copy(dz):
        return pltpu.make_async_remote_copy(
            rawall.at[0], rawall.at[g.at(-dz)], raw_send, raw_recv,
            device_id=(chip(y, zmod(z + dz), x), c), device_id_type=MESH,
        )

    for dz in range(1, g.nz):
        raw_copy(dz).start()

    def hops(number, way):
        return hops_of(number, way, g.nz // 2)

    def lanes(q):
        return pl.ds(g.starts[q], g.ahead[q])

    def z_copy(q, way, step):
        sign = 1 - 2 * way
        src = xall.at[g.at(-sign * (step - 1)), :, lanes(q)]
        dst = xall.at[g.at(-sign * step), :, lanes(q)]
        return pltpu.make_async_remote_copy(
            src, dst, z_send, z_recv.at[q, way, step - 1],
            device_id=(chip(y, zmod(z + sign), x), c), device_id_type=MESH,
        )

    pltpu.make_async_copy(tok_hbm, xall.at[0], own_sem).wait()

    def tables():
        pltpu.make_async_copy(rawall.at[pl.ds(1, g.nz - 1)], rawall.at[pl.ds(1, g.nz - 1)], raw_recv).wait()
        lane = lax.broadcasted_iota(jnp.int32, (2 * g.top, LANES), 1)
        pairs = [
            jnp.where(lane < g.tok, rawall[2 * p], rawall[2 * p + 1]) for p in range(g.nz // 2)
        ]
        raw = jnp.concatenate(pairs, axis=1)
        place = lax.broadcasted_iota(jnp.int32, (g.xy, g.col), 0)
        named_by = (((place // g.nx) * g.nz + z) * g.nx + lax.rem(place, g.nx)).astype(F32)
        named = jnp.zeros((g.xy, g.col), F32)
        weight = jnp.zeros((g.xy, g.col), F32)
        for k in range(g.top):
            hit = raw[k:k + 1, :] == named_by
            named = named + jnp.where(hit, 1.0, 0.0)
            weight = weight + jnp.where(hit, raw[g.top + k:g.top + k + 1, :], 0.0)
        early = lax.broadcasted_iota(jnp.int32, (g.col, g.col), 0)
        late = lax.broadcasted_iota(jnp.int32, (g.col, g.col), 1)
        before = jnp.where((early // g.tok == late // g.tok) & (early < late), 1.0, 0.0).astype(BF16)
        rank = nn(named.astype(BF16), before)
        token = lax.broadcasted_iota(jnp.int32, (g.xy, g.col), 1)
        key = jnp.where(named > 0.0, rank + (CAP * (token // g.tok)).astype(F32), -1.0)
        slot = lax.broadcasted_iota(jnp.int32, (g.slots, g.col), 0).astype(F32)
        for d in range(g.xy):
            hit = key[d:d + 1, :] == slot
            pick[d * g.slots:(d + 1) * g.slots, :] = jnp.where(hit, 1.0, 0.0).astype(BF16)
            scaled[d * g.slots:(d + 1) * g.slots, :] = jnp.where(hit, weight[d:d + 1, :], 0.0).astype(BF16)

        whole = pick[...].reshape(g.xy, g.slots, g.col)
        pick_near[...] = whole[:, :g.early, :g.reach * g.tok].reshape(g.xy * g.early, g.reach * g.tok)
        late_slots = g.slots - g.early
        pick_far[...] = whole[:, g.early:, (g.reach - 1) * g.tok:].reshape(g.xy * late_slots, g.col - (g.reach - 1) * g.tok)

    mine = y * (g.nx // 2) + x // 2

    def to_plane(rows, span, sem, off):
        yy = lax.rem(y + off // g.nx, g.ny)
        xx = lax.rem(x + lax.rem(off, g.nx), g.nx)
        src = sbuf.at[yy * g.nx + xx, rows, span]
        dst = rbuf.at[c, mine, rows, span]
        stays = (off == 0) & (parity == c)

        @pl.when(jnp.logical_not(stays))
        def _():
            pltpu.make_async_remote_copy(
                src, dst, xy_send, sem, device_id=(chip(yy, z, xx), parity), device_id_type=MESH
            ).start()

        @pl.when(stays)
        def _():
            pltpu.make_async_copy(src, dst, sem).start()

    early_rows, late_rows = pl.ds(0, g.early), pl.ds(g.early, g.slots - g.early)

    def near_span(n):
        return g.starts[g.near[n][0]], sum(g.ahead[q] for q in g.near[n])

    def gather_near(n):
        start, width = near_span(n)
        rows = xall[:g.reach, :, start:start + width].reshape(g.reach * g.tok, width)
        got = nn(pick_near[...], rows).astype(BF16)
        sbuf[:, :g.early, start:start + width] = got.reshape(g.xy, g.early, width)

        @pl.loop(0, g.xy)
        def _(off):
            to_plane(early_rows, pl.ds(start, width), near_recv.at[c, n], off)

    def gather_far(q):
        start, width = g.starts[q], g.ahead[q]
        rows = xall[g.reach - 1:, :, start:start + width].reshape(g.col - (g.reach - 1) * g.tok, width)
        groups = 4
        per = g.xy // groups
        late = g.slots - g.early
        for i in range(groups):
            got = nn(pick_far[i * per * late:(i + 1) * per * late, :], rows).astype(BF16)
            sbuf[i * per:(i + 1) * per, g.early:, start:start + width] = got.reshape(per, late, width)

        @pl.loop(0, g.xy)
        def _(off):
            to_plane(late_rows, pl.ds(start, width), xy_recv.at[c, q], off)

    arrived = set()

    def need(q, steps):
        for at in steps:
            for way in range(2):
                if at <= hops(q, way) and (q, way, at) not in arrived:
                    arrived.add((q, way, at))
                    z_copy(q, way, at).wait_recv()

    def need_one(q, way, at):
        if at and (q, way, at) not in arrived:
            arrived.add((q, way, at))
            z_copy(q, way, at).wait_recv()

    swapped = False
    for step in ring_plan(g.ahead, g.near, g.nz // 2):
        if step[0] == "send":
            _, q, way, at = step
            need_one(q, way, at - 1)
            z_copy(q, way, at).start()
        elif step[0] == "tables":
            tables()
        elif step[0] == "near":
            for q in g.near[step[1]]:
                need(q, (1,))
            gather_near(step[1])
            if not swapped:
                swapped = True
                for i in range(3):
                    weight_own(i).wait()
                    weight_swap(i).start()
        else:
            need(step[1], range(1, g.nz // 2 + 1))
            gather_far(step[1])

    early = lax.broadcasted_iota(jnp.int32, (g.col, g.col), 0)
    late = lax.broadcasted_iota(jnp.int32, (g.col, g.col), 1)
    same = jnp.where(early == late, 1.0, 0.0).astype(BF16)
    pick_t[...] = nt(same, pick[...]).astype(BF16)
    whole = scaled[...].reshape(g.xy, g.slots, g.col)
    near_cols, far_cols = g.reach * g.tok, g.col - (g.reach - 1) * g.tok
    near_t[...] = nt(same[:near_cols, :near_cols], whole[:, :g.early, :near_cols].reshape(g.xy * g.early, near_cols)).astype(BF16)
    far_slots = whole[:, g.early:, g.col - far_cols:].reshape(g.xy * (g.slots - g.early), far_cols)
    far_t[...] = nt(same[:far_cols, :far_cols], far_slots).astype(BF16)

    for i in range(3):
        weight_swap(i).wait()

    for q in range(g.nq):
        feats = slice(g.starts[q], g.starts[q] + g.ahead[q])
        for n, group in enumerate(g.near):
            if q == group[0]:
                start, width = near_span(n)
                for kind in range(2):
                    came = rbuf.at[kind, :, early_rows, pl.ds(start, width)]
                    pltpu.make_async_copy(came, came, near_recv.at[kind, n]).wait()
        for kind in range(2):
            came = rbuf.at[kind, :, late_rows, lanes(q)]
            pltpu.make_async_copy(came, came, xy_recv.at[kind, q]).wait()
        rows = rbuf[0, :, :, feats].reshape(g.rows, g.ahead[q])
        grads = rbuf[1, :, :, feats].reshape(g.rows, g.ahead[q])
        if q == 0:
            gacc[...] = nn(rows, wg[feats, :])
            uacc[...] = nn(rows, wu[feats, :])
            hacc[...] = nt(grads, wd[:, feats])
        else:
            gacc[...] += nn(rows, wg[feats, :])
            uacc[...] += nn(rows, wu[feats, :])
            hacc[...] += nt(grads, wd[:, feats])

    for i in range(g.src):
        span = slice(i * g.slots, (i + 1) * g.slots)
        gate_pre, up_pre, grad_hidden = gacc[span, :], uacc[span, :], hacc[span, :]
        sigma = jax.nn.sigmoid(gate_pre)
        down = grad_hidden * (gate_pre * sigma)
        score = jnp.sum(down * up_pre, axis=1, keepdims=True)
        wide = jnp.broadcast_to(score, (g.slots, LANES)).astype(BF16)
        first = jnp.where(lax.broadcasted_iota(jnp.int32, (16, LANES), 1) == 0, 1.0, 0.0).astype(BF16)
        ret[0][0, i, :, :g.slots] = nt(first, wide).astype(BF16)
        gu[span, :] = down.astype(BF16)
        gg[span, :] = (grad_hidden * up_pre * sigma * (1.0 + gate_pre * (1.0 - sigma))).astype(BF16)

    here_d = y * g.nx + x

    def to_source(j, h, i, rows, sem):
        dy = i // (g.nx // 2)
        dx = 2 * lax.rem(i, g.nx // 2) + lax.rem(dy + parity + c, 2)
        yy = lax.rem(y + dy, g.ny)
        xx = lax.rem(x + dx, g.nx)
        src = ret[j].at[h if j else 0, yy * (g.nx // 2) + xx // 2, rows]
        dst = back[j].at[here_d, rows]
        stays = (xx == x) & (yy == y) & (c == h)

        @pl.when(jnp.logical_not(stays))
        def _():
            pltpu.make_async_remote_copy(
                src, dst, ret_send.at[j], sem, device_id=(chip(yy, z, xx), h), device_id_type=MESH
            ).start()

        @pl.when(stays)
        def _():
            pltpu.make_async_copy(src, dst, sem).start()

    def send_back(j, rows, sem):
        @pl.loop(0, g.src)
        def _(i):
            for h in range(2):
                to_source(j, h, i, rows, sem)

    def make(j):
        w = g.widths[j]
        if j:
            cuts = [h * g.dh + g.cuts[j] for h in range(2)]
            both = [jnp.concatenate([ref[cut:cut + w, :] for cut in cuts], axis=0) for ref in (wg, wu)]
            got = (nt(gg[...], both[0]) + nt(gu[...], both[1])).astype(BF16)
            for h in range(2):
                ret[j][h] = got[:, h * w:(h + 1) * w].reshape(g.src, g.slots, w)

        send_back(j, late_rows if j else pl.ds(0, 16), ret_recv.at[j])

    def combine(j):
        came = back[j].at[:, late_rows if j else pl.ds(0, 16)]
        pltpu.make_async_copy(came, came, ret_recv.at[j]).wait()
        if j == 0:
            slot = lax.broadcasted_iota(jnp.int32, (g.slots, g.slots), 0)
            same = jnp.where(slot == lax.broadcasted_iota(jnp.int32, (g.slots, g.slots), 1), 1.0, 0.0).astype(BF16)
            at = lax.broadcasted_iota(jnp.int32, (g.slots, LANES), 1)
            placed = []
            for d in range(g.xy):
                column = nt(same, back[0][d, :, :g.slots])[:, :1]
                expert = ((d // g.nx) * g.nz + z) * g.nx + d % g.nx
                placed.append(jnp.where(at == expert, column, 0.0).astype(BF16))
            part[0][...] = nn(pick_t[...], jnp.concatenate(placed, axis=0))
        else:
            late = g.slots - g.early
            part[j][(g.reach - 1) * g.tok:, :] = nn(far_t[...], back[j][:, g.early:, :].reshape(g.xy * late, g.widths[j]))

    def combine_near(j):
        came = back[j].at[:, early_rows]
        pltpu.make_async_copy(came, came, back_recv.at[j]).wait()
        got = nn(near_t[...], back[j][:, :g.early, :].reshape(g.xy * g.early, g.widths[j]))
        edge = (g.reach - 1) * g.tok
        part[j][:edge, :] = got[:edge]
        part[j][edge:edge + g.tok, :] += got[edge:]

    def own_part(j, away):
        block = g.at(away)
        return part[j][block * g.tok:(block + 1) * g.tok, :]

    def spot(j, way, step):
        return step - 1 + way * hops(j, 0)

    def rs_copy(j, way, step):
        sign = 1 - 2 * way
        n = spot(j, way, step)
        return pltpu.make_async_remote_copy(
            rsend[j].at[n], rrecv[j].at[n], rs_send.at[j], rs_recv.at[j, n],
            device_id=(chip(y, zmod(z + sign), x), c), device_id_type=MESH,
        )

    def rs_step(j, step, last):
        for way in range(2):
            n = hops(j, way)
            at = n if last else step
            if at > n or (at == n and j and not last):
                continue
            sign = 1 - 2 * way
            term = own_part(j, sign * (n + 1 - at))
            if at > 1:
                rs_copy(j, way, at - 1).wait_recv()
                term = term + rrecv[j][spot(j, way, at - 1)].astype(F32)
            rsend[j][spot(j, way, at)] = term.astype(BF16)
            rs_copy(j, way, at).start()

    def rs_direct(j, away, sem):
        for dz in away:
            rsend[j][dz - 1] = own_part(j, dz).astype(BF16)
            pltpu.make_async_remote_copy(
                rsend[j].at[dz - 1], rrecv[j].at[dz - 1], rs_send.at[j], rs_recv.at[j, sem + (dz == g.nz - 1)],
                device_id=(chip(y, zmod(z + dz), x), c), device_id_type=MESH,
            ).start()

    far_away = sorted(range(2, g.nz - 1), key=lambda v: -min(v, g.nz - v))

    def swap(j):
        span = pl.ds(pl.multiple_of(c * g.dh + g.cuts[j], LANES), g.widths[j])
        return pltpu.make_async_remote_copy(
            out_ref.at[:, span], out_ref.at[:, span], out_send, out_recv,
            device_id=(e, other), device_id_type=MESH,
        )

    def rs_last(j):
        total = own_part(j, 0)
        if j in g.direct:
            for n, some in enumerate((pl.ds(1, g.nz - 3), pl.ds(0, 1), pl.ds(g.nz - 2, 1))):
                pltpu.make_async_copy(rrecv[j].at[some], rrecv[j].at[some], rs_recv.at[j, n]).wait()
            for n in range(g.nz - 1):
                total = total + rrecv[j][n].astype(F32)
        else:
            for way in range(2):
                rs_copy(j, way, hops(j, way)).wait_recv()
                total = total + rrecv[j][spot(j, way, hops(j, way))].astype(F32)
        if j:
            out_ref[:, pl.ds(pl.multiple_of(c * g.dh + g.cuts[j], LANES), g.widths[j])] = total.astype(BF16)
            swap(j).start()
        else:
            square = (LANES, LANES)
            same = lax.broadcasted_iota(jnp.int32, square, 0) == lax.broadcasted_iota(jnp.int32, square, 1)
            scores = nt(jnp.where(same, 1.0, 0.0).astype(BF16), total.astype(BF16))
            expert_at = lax.broadcasted_iota(jnp.int32, (LANES, g.tok), 0)
            for k in range(g.top):
                one = jnp.where(expert_at == ids_ref[k:k + 1, :], scores, 0.0)
                gate_ref[k:k + 1, :] = jnp.sum(one, axis=0, keepdims=True)

    for kind, j, *step in sum_plan(g.widths, g.nz // 2, g.direct, g.early / g.slots):
        if kind == "make":
            make(j)
        elif kind == "near":
            send_back(j, early_rows, back_recv.at[j])
        elif kind == "combine":
            combine(j)
            if j in g.direct:
                rs_direct(j, far_away, 0)
            else:
                rs_step(j, 1, False)
        elif kind == "add":
            rs_step(j, step[0] + 1, False)
        elif kind == "close":
            combine_near(j)
            if j in g.direct:
                rs_direct(j, (1, g.nz - 1), 1)
            else:
                rs_step(j, 0, True)
        else:
            rs_last(j)

    def gone(ref, sem):
        pltpu.make_async_copy(ref, ref, sem).wait()

    some = pl.ds(0, g.nz - 1)
    gone(rawall.at[some], raw_send)
    gone(xall.at[some], z_send)
    for j in range(g.nj):
        gone(rsend[j], rs_send.at[j])

    @pl.when(parity == c)
    def _():
        fewer = pl.ds(0, g.xy - 1)
        gone(sbuf.at[fewer], xy_send)
        for j in range(g.nj):
            gone(back[j].at[fewer], ret_send.at[j])

    @pl.when(parity != c)
    def _():
        gone(sbuf, xy_send)
        for j in range(g.nj):
            gone(back[j], ret_send.at[j])

    half = out_ref.at[:, pl.ds(0, g.dh)]
    gone(half, out_send)
    gone(half, out_recv)


def scratch(g):
    dma = pltpu.SemaphoreType.DMA
    half = g.nz // 2
    vm = pltpu.VMEM
    return [
        vm((g.top, g.tok), jnp.int32),
        vm((g.top, g.tok), F32),
        vm((g.nz, g.tok, g.dim), BF16),
        vm((g.nz, 2 * g.top, LANES), F32),
        vm((g.xy * g.early, g.reach * g.tok), BF16),
        vm((g.xy * (g.slots - g.early), g.col - (g.reach - 1) * g.tok), BF16),
        vm((g.all_slots, g.col), BF16),
        vm((g.all_slots, g.col), BF16),
        vm((g.col, g.all_slots), BF16),
        vm((g.reach * g.tok, g.xy * g.early), BF16),
        vm((g.col - (g.reach - 1) * g.tok, g.xy * (g.slots - g.early)), BF16),
        vm((g.xy, g.slots, g.dim), BF16),
        vm((2, g.src, g.slots, g.dim), BF16),
        vm((g.dim, g.ff), BF16),
        vm((g.dim, g.ff), BF16),
        vm((g.ff, g.dim), BF16),
        vm((g.rows, g.ff), F32),
        vm((g.rows, g.ff), F32),
        vm((g.rows, g.ff), F32),
        vm((g.rows, g.ff), BF16),
        vm((g.rows, g.ff), BF16),
        dma((2,)),
        dma(()),
        dma((3,)),
        dma((3,)),
        dma((3,)),
        dma(()),
        dma(()),
        dma(()),
        dma((g.nq, 2, half)),
        dma(()),
        dma((2, len(g.near))),
        dma((2, g.nq)),
        dma((g.nj,)),
        dma((g.nj,)),
        dma((g.nj,)),
        dma((g.nj,)),
        dma((g.nj, g.nz - 1)),
        dma(()),
        dma(()),
        *[vm((2 if j else 1, g.src, g.slots if j else 16, w), BF16) for j, w in enumerate(g.widths)],
        *[vm((g.xy, g.slots if j else 16, w), BF16) for j, w in enumerate(g.widths)],
        *[vm((g.col, w), F32) for w in g.widths],
        *[vm((g.nz - 1, g.tok, w), BF16) for w in g.widths],
        *[vm((g.nz - 1, g.tok, w), BF16) for w in g.widths],
    ]


def per_device(ny, nz, nx, ahead, near, widths, direct, tokens, cotangent, expert_ids, gate_weights, w_gate, w_up, w_down):
    tok, dim = tokens.shape
    top = expert_ids.shape[1]
    g = Sizes(tok, dim, w_gate.shape[2], top, ny, nz, nx, ahead, near, widths, direct)
    vmem = pl.BlockSpec(memory_space=pltpu.VMEM)
    hbm = pl.BlockSpec(memory_space=pl.ANY)
    input_grad, gate_grad = pl.pallas_call(
        functools.partial(kernel, g),
        out_shape=(
            pltpu.VMEM((tok, dim), BF16),
            pltpu.VMEM((top, tok), F32),
        ),
        in_specs=[hbm] * 7,
        out_specs=(vmem, vmem),
        scratch_shapes=scratch(g),
        compiler_params=pltpu.CompilerParams(
            collective_id=0, has_side_effects=True, vmem_limit_bytes=60 * 1024 * 1024
        ),
    )(expert_ids.T, gate_weights.T, tokens, cotangent, w_gate, w_up, w_down)
    return input_grad, gate_grad.T.astype(BF16)


def solution(mesh, ny=NY, nz=NZ, nx=NX, ahead=(256,) * 8, near=((0,), (1,), (2, 3), (4, 5), (6, 7)), widths=(LANES, 256, 256, 256, 256), direct=()):
    placed = (
        P("expert", None),
        P("expert", None),
        P("expert", None),
        P("expert", None),
        P("expert", None, "half"),
        P("expert", None, "half"),
        P("expert", "half", None),
    )
    return jax.shard_map(
        functools.partial(per_device, ny, nz, nx, ahead, near, widths, direct),
        mesh=mesh,
        in_specs=placed,
        out_specs=(P("expert", None), P("expert", None)),
        check_vma=False,
    )
```

time: 106 us -> 89.4 us (0.84); the launches traced: 105 us -> 89.3 us
  Pallas kernels: 101 us -> 87.4 us
    pallas_call x1, Pallas kernels: 101 us -> 87.4 us  [per_device(): pl.pallas_call(functools.partial(kernel, g), out_shape=(pltpu.VMEM((tok,...]
where the time goes in v3:
time: 89.4 us; the launch traced here: 89.3 us
  Pallas kernels  87.4 us (98%)
    pallas_call x1, Pallas kernels, per_device(): pl.pallas_call(functools.partial(kernel, g), out_shape=(pltpu.VMEM((tok,...  87.4 us

profile of v3, /device:TPU:1, one launch (start us, length us, event | category | flops | bytes accessed | tf_op | source)
XLA Modules:
  0.0 89.3 jit_solution(16564512677703498487)
XLA Ops:
  0.6 87.4 %shard_map.86 = (bf16[64,2048]{1,0:T(8,128)(2,1)S(1)}, f32[8,64]{1,0:T(8,128)S(1)}) custom-call(s32[8,64]{1,0:T(8,128)} %bitcast.4, f32[8,64]{1,0:T(8,128)} %bitcast.5, bf16[64,2048]{1,0:T(8,128)(2,1)} %tok_hbm.1, bf16[64,2048]{1,0:T(8,128)(2,1)} %cot_hbm.1, bf16[1,2048,384]{2,1,0:T(8,128)(2,1)} %wg_hbm.1, bf16[1,2048,384]{2,1,0:T(8,128)(2,1)} %wu_hbm.1, ...), custom_call_target="tpu_custom_call" | custom-call | tf_op jit(solution)/shard_map/pallas_call | solution.py:621
  88.0 0.7 copy.10
  88.7 0.6 convert_bitcast_fusion

commit v4 on v3

--- a/solution.py
+++ b/solution.py
@@ -27,7 +27,7 @@
     def at(self, away):
         return self.order.index(away % self.nz)
 
-    def __init__(self, tok, dim, half_ff, top, ny, nz, nx, ahead, near, widths, direct):
+    def __init__(self, tok, dim, half_ff, top, ny, nz, nx, ahead, near, widths):
         self.tok, self.dim, self.hf, self.ff, self.top = tok, dim, half_ff, 2 * half_ff, top
         self.ny, self.nz, self.nx = ny, nz, nx
         self.ahead = ahead
@@ -37,6 +37,9 @@
         self.order = [0] + [v for k in range(1, nz // 2) for v in (k, nz - k)] + [nz // 2]
         self.early = 16
         self.reach = 3
+        self.tiers = [
+            (low, low + 16, low // CAP, (low + 15) // CAP + 1) for low in range(0, CAP * nz, 16)
+        ]
         self.xy = ny * nx
         self.src = self.xy // 2
         self.slots = CAP * nz
@@ -47,7 +50,6 @@
         self.widths = widths
         self.cuts = [sum(widths[1:j]) for j in range(len(widths))]
         self.nj = len(widths)
-        self.direct = direct
 
 
 def hops_of(number, way, half):
@@ -77,59 +79,62 @@
             came[q, way, step] = link + lag
             if step < hops_of(q, way, half):
                 ready[q, step + 1] = link + lag
-    events = [(4.4, 1, "tables")]
+    events = [(2.9, 1, "tables"), (6.6, 1, "tables_far")]
     first = [max(came[q, way, 1] for q in group for way in range(2)) for group in near]
-    events += [(max(4.9, t), 2, "near", n) for n, t in enumerate(first)]
-    latest = max(4.9, max(first))
+    events += [(max(3.1, t), 2, "near", n) for n, t in enumerate(first)]
+    latest = max(6.7, max(first))
     for q in range(len(widths)):
         t = max(v for k, v in came.items() if k[0] == q)
         events.append((max(t, latest + 0.01), 3, "far", q))
     return [event[2:] for event in sorted(sends + events)]
 
 
-def sum_plan(widths, half, direct, early):
+def sum_plan(widths, half):
     count = len(widths)
-    plan, events, now, plane, link = [], [], 0.0, 0.0, 0.0
+    plan, events, here, link = [], [], {}, 0.0
+    clock = [0.0, 0.0]
+
+    def issue(kind, j, cost, arrival, lanes):
+        plan.append((kind, j))
+        clock[0] += cost
+        clock[1] = max(clock) + 0.0168 * lanes
+        here[arrival, j] = clock[1] + 3.8
+
     for j in [1, 0, *range(2, count)]:
-        plan.append(("make", j))
-        now += 1.8 if j else 0.4
-        plane = max(plane, now) + (0.0168 * widths[j] * (1.0 - early) if j else 0.7)
-        events.append((plane + 3.8, "combine", j, 0))
-    close = [0.0] * count
+        issue("make", j, 1.8 if j else 0.4, "combine", widths[j] / 3)
+        if j == 1:
+            issue("middle", 1, 0.4, "mid", widths[1] / 3)
+    for j in range(2, count):
+        issue("middle", j, 0.4, "mid", widths[j] / 3)
     for j in range(1, count):
-        plan.append(("near", j))
-        now += 0.4
-        plane = max(plane, now) + 0.0168 * widths[j] * early
-        close[j] = plane + 3.8
+        issue("near", j, 0.4, "close", widths[j] / 3)
+    events = [(here["combine", j], "combine", j, 0) for j in range(count)]
+    now = clock[0]
     while events:
         at, kind, j, step = min(events)
         events.remove((at, kind, j, step))
         now = max(now, at)
         plan.append((kind, j, step))
-        now += {"combine": 0.5, "add": 0.25, "close": 0.6, "last": 0.3}[kind]
+        now += {"combine": 0.4, "mid": 0.5, "add": 0.25, "close": 0.6, "last": 0.3}[kind]
         if kind == "last":
             continue
-        if j in direct:
-            units = 7.0 if kind == "combine" else 1.0
+        link = max(link, now) + 0.0036 * widths[j]
+        there = link + 2.3
+        if kind == "close" or (j == 0 and step == half - 1):
+            events.append((there, "last", j, 0))
+        elif j == 0:
+            events.append((there, "add", j, step + 1))
         else:
-            units = 1.0
-        link = max(link, now) + 0.0036 * units * widths[j]
-        there = link + (4.1 if j in direct and kind == "combine" else 2.3)
-        hops = half if j == 0 else half - 1
-        if kind == "close" or (j == 0 and step == hops - 1):
-            events.append((there, "last", j, 0))
-        elif j in direct or step == hops - 1:
-            events.append((close[j] if j in direct else max(close[j], there), "close", j, 0))
-        else:
-            events.append((there, "add", j, step + 1))
+            after = {"combine": "mid", "mid": "add", "add": "close"}[kind]
+            events.append((max(there, here.get((after, j), 0.0)), after, j, 0))
     return plan
 
 
 def kernel(
     g, ids_hbm, gates_hbm, tok_hbm, cot_hbm, wg_hbm, wu_hbm, wd_hbm, out_ref, gate_ref,
-    ids_ref, gates_ref, xall, rawall, pick_near, pick_far, pick, scaled, pick_t, near_t, far_t, sbuf, rbuf, wg, wu, wd, gacc, uacc, hacc, gg, gu,
+    ids_ref, gates_ref, xall, rawall, pick_near, pick_far, pick, scaled, pick_t, near_t, mid_t, far_t, sbuf, rbuf, wg, wu, wd, gacc, uacc, hacc, gg, gu,
     table_sem, own_sem, w_own_sem, w_send, w_recv, raw_send, raw_recv, z_send, z_recv, xy_send, near_recv, xy_recv,
-    ret_send, ret_recv, back_recv, rs_send, rs_recv, out_send, out_recv, *lists,
+    ret_send, ret_recv, mid_recv, back_recv, rs_send, rs_recv, out_send, out_recv, *lists,
 ):
     ret, back, part, rsend, rrecv = (lists[k * g.nj:(k + 1) * g.nj] for k in range(5))
     e = lax.axis_index("expert")
@@ -192,11 +197,11 @@
 
     def raw_copy(dz):
         return pltpu.make_async_remote_copy(
-            rawall.at[0], rawall.at[g.at(-dz)], raw_send, raw_recv,
+            rawall.at[0], rawall.at[g.at(-dz)], raw_send, raw_recv.at[g.at(-dz) // 4],
             device_id=(chip(y, zmod(z + dz), x), c), device_id_type=MESH,
         )
 
-    for dz in range(1, g.nz):
+    for dz in sorted(range(1, g.nz), key=lambda v: g.at(-v)):
         raw_copy(dz).start()
 
     def hops(number, way):
@@ -216,37 +221,48 @@
 
     pltpu.make_async_copy(tok_hbm, xall.at[0], own_sem).wait()
 
-    def tables():
-        pltpu.make_async_copy(rawall.at[pl.ds(1, g.nz - 1)], rawall.at[pl.ds(1, g.nz - 1)], raw_recv).wait()
+    def keys(count):
         lane = lax.broadcasted_iota(jnp.int32, (2 * g.top, LANES), 1)
-        pairs = [
-            jnp.where(lane < g.tok, rawall[2 * p], rawall[2 * p + 1]) for p in range(g.nz // 2)
-        ]
+        pairs = [jnp.where(lane < g.tok, rawall[2 * p], rawall[2 * p + 1]) for p in range(count // 2)]
         raw = jnp.concatenate(pairs, axis=1)
-        place = lax.broadcasted_iota(jnp.int32, (g.xy, g.col), 0)
+        col = count * g.tok
+        place = lax.broadcasted_iota(jnp.int32, (g.xy, col), 0)
         named_by = (((place // g.nx) * g.nz + z) * g.nx + lax.rem(place, g.nx)).astype(F32)
-        named = jnp.zeros((g.xy, g.col), F32)
-        weight = jnp.zeros((g.xy, g.col), F32)
+        named = jnp.zeros((g.xy, col), F32)
+        weight = jnp.zeros((g.xy, col), F32)
         for k in range(g.top):
             hit = raw[k:k + 1, :] == named_by
             named = named + jnp.where(hit, 1.0, 0.0)
             weight = weight + jnp.where(hit, raw[g.top + k:g.top + k + 1, :], 0.0)
-        early = lax.broadcasted_iota(jnp.int32, (g.col, g.col), 0)
-        late = lax.broadcasted_iota(jnp.int32, (g.col, g.col), 1)
+        early = lax.broadcasted_iota(jnp.int32, (col, col), 0)
+        late = lax.broadcasted_iota(jnp.int32, (col, col), 1)
         before = jnp.where((early // g.tok == late // g.tok) & (early < late), 1.0, 0.0).astype(BF16)
         rank = nn(named.astype(BF16), before)
-        token = lax.broadcasted_iota(jnp.int32, (g.xy, g.col), 1)
-        key = jnp.where(named > 0.0, rank + (CAP * (token // g.tok)).astype(F32), -1.0)
+        token = lax.broadcasted_iota(jnp.int32, (g.xy, col), 1)
+        return jnp.where(named > 0.0, rank + (CAP * (token // g.tok)).astype(F32), -1.0), weight
+
+    def tables():
+        came = rawall.at[pl.ds(1, 3)]
+        pltpu.make_async_copy(came, came, raw_recv.at[0]).wait()
+        key, _ = keys(4)
+        width = g.reach * g.tok
+        slot = lax.broadcasted_iota(jnp.int32, (g.early, width), 0).astype(F32)
+        for d in range(g.xy):
+            hit = key[d:d + 1, :width] == slot
+            pick_near[d * g.early:(d + 1) * g.early, :] = jnp.where(hit, 1.0, 0.0).astype(BF16)
+
+    def tables_far():
+        came = rawall.at[pl.ds(4, g.nz - 4)]
+        pltpu.make_async_copy(came, came, raw_recv.at[1]).wait()
+        key, weight = keys(g.nz)
         slot = lax.broadcasted_iota(jnp.int32, (g.slots, g.col), 0).astype(F32)
         for d in range(g.xy):
             hit = key[d:d + 1, :] == slot
             pick[d * g.slots:(d + 1) * g.slots, :] = jnp.where(hit, 1.0, 0.0).astype(BF16)
             scaled[d * g.slots:(d + 1) * g.slots, :] = jnp.where(hit, weight[d:d + 1, :], 0.0).astype(BF16)
-
-        whole = pick[...].reshape(g.xy, g.slots, g.col)
-        pick_near[...] = whole[:, :g.early, :g.reach * g.tok].reshape(g.xy * g.early, g.reach * g.tok)
         late_slots = g.slots - g.early
-        pick_far[...] = whole[:, g.early:, (g.reach - 1) * g.tok:].reshape(g.xy * late_slots, g.col - (g.reach - 1) * g.tok)
+        late = pick[...].reshape(g.xy, g.slots, g.col)[:, g.early:, (g.reach - 1) * g.tok:]
+        pick_far[...] = late.reshape(g.xy * late_slots, g.col - (g.reach - 1) * g.tok)
 
     mine = y * (g.nx // 2) + x // 2
 
@@ -318,6 +334,8 @@
             z_copy(q, way, at).start()
         elif step[0] == "tables":
             tables()
+        elif step[0] == "tables_far":
+            tables_far()
         elif step[0] == "near":
             for q in g.near[step[1]]:
                 need(q, (1,))
@@ -336,10 +354,10 @@
     same = jnp.where(early == late, 1.0, 0.0).astype(BF16)
     pick_t[...] = nt(same, pick[...]).astype(BF16)
     whole = scaled[...].reshape(g.xy, g.slots, g.col)
-    near_cols, far_cols = g.reach * g.tok, g.col - (g.reach - 1) * g.tok
-    near_t[...] = nt(same[:near_cols, :near_cols], whole[:, :g.early, :near_cols].reshape(g.xy * g.early, near_cols)).astype(BF16)
-    far_slots = whole[:, g.early:, g.col - far_cols:].reshape(g.xy * (g.slots - g.early), far_cols)
-    far_t[...] = nt(same[:far_cols, :far_cols], far_slots).astype(BF16)
+    for ref, (low, high, first, last) in ((near_t, g.tiers[0]), (mid_t, g.tiers[1]), (far_t, g.tiers[2])):
+        cols = (last - first) * g.tok
+        rows = whole[:, low:high, first * g.tok:last * g.tok].reshape(g.xy * (high - low), cols)
+        ref[...] = nt(same[:cols, :cols], rows).astype(BF16)
 
     for i in range(3):
         weight_swap(i).wait()
@@ -399,6 +417,9 @@
         def _():
             pltpu.make_async_copy(src, dst, sem).start()
 
+    def tier_rows(n):
+        return pl.ds(g.tiers[n][0], g.tiers[n][1] - g.tiers[n][0])
+
     def send_back(j, rows, sem):
         @pl.loop(0, g.src)
         def _(i):
@@ -414,10 +435,10 @@
             for h in range(2):
                 ret[j][h] = got[:, h * w:(h + 1) * w].reshape(g.src, g.slots, w)
 
-        send_back(j, late_rows if j else pl.ds(0, 16), ret_recv.at[j])
+        send_back(j, tier_rows(2) if j else pl.ds(0, 16), ret_recv.at[j])
 
     def combine(j):
-        came = back[j].at[:, late_rows if j else pl.ds(0, 16)]
+        came = back[j].at[:, tier_rows(2) if j else pl.ds(0, 16)]
         pltpu.make_async_copy(came, came, ret_recv.at[j]).wait()
         if j == 0:
             slot = lax.broadcasted_iota(jnp.int32, (g.slots, g.slots), 0)
@@ -430,16 +451,21 @@
                 placed.append(jnp.where(at == expert, column, 0.0).astype(BF16))
             part[0][...] = nn(pick_t[...], jnp.concatenate(placed, axis=0))
         else:
-            late = g.slots - g.early
-            part[j][(g.reach - 1) * g.tok:, :] = nn(far_t[...], back[j][:, g.early:, :].reshape(g.xy * late, g.widths[j]))
-
-    def combine_near(j):
-        came = back[j].at[:, early_rows]
-        pltpu.make_async_copy(came, came, back_recv.at[j]).wait()
-        got = nn(near_t[...], back[j][:, :g.early, :].reshape(g.xy * g.early, g.widths[j]))
-        edge = (g.reach - 1) * g.tok
-        part[j][:edge, :] = got[:edge]
-        part[j][edge:edge + g.tok, :] += got[edge:]
+            got, first, _ = tier_sum(j, far_t, 2)
+            part[j][first * g.tok:, :] = got
+
+    def tier_sum(j, weights, n):
+        low, high, first, last = g.tiers[n]
+        rows = back[j][:, low:high, :].reshape(g.xy * (high - low), g.widths[j])
+        return nn(weights[...], rows), first, last
+
+    def combine_more(j, weights, n, sem):
+        came = back[j].at[:, tier_rows(n)]
+        pltpu.make_async_copy(came, came, sem).wait()
+        got, first, last = tier_sum(j, weights, n)
+        edge = (last - 1 - first) * g.tok
+        part[j][first * g.tok:(last - 1) * g.tok, :] = got[:edge]
+        part[j][(last - 1) * g.tok:last * g.tok, :] += got[edge:]
 
     def own_part(j, away):
         block = g.at(away)
@@ -456,29 +482,33 @@
             device_id=(chip(y, zmod(z + sign), x), c), device_id_type=MESH,
         )
 
-    def rs_step(j, step, last):
+    passed = {}
+
+    def rs_next(j, way):
+        n = hops(j, way)
+        at = passed.get((j, way), 0) + 1
+        passed[j, way] = at
+        sign = 1 - 2 * way
+        term = own_part(j, sign * (n + 1 - at))
+        if at > 1:
+            rs_copy(j, way, at - 1).wait_recv()
+            term = term + rrecv[j][spot(j, way, at - 1)].astype(F32)
+        rsend[j][spot(j, way, at)] = term.astype(BF16)
+        rs_copy(j, way, at).start()
+
+    def rs_move(j, kind):
         for way in range(2):
-            n = hops(j, way)
-            at = n if last else step
-            if at > n or (at == n and j and not last):
-                continue
-            sign = 1 - 2 * way
-            term = own_part(j, sign * (n + 1 - at))
-            if at > 1:
-                rs_copy(j, way, at - 1).wait_recv()
-                term = term + rrecv[j][spot(j, way, at - 1)].astype(F32)
-            rsend[j][spot(j, way, at)] = term.astype(BF16)
-            rs_copy(j, way, at).start()
-
-    def rs_direct(j, away, sem):
-        for dz in away:
-            rsend[j][dz - 1] = own_part(j, dz).astype(BF16)
-            pltpu.make_async_remote_copy(
-                rsend[j].at[dz - 1], rrecv[j].at[dz - 1], rs_send.at[j], rs_recv.at[j, sem + (dz == g.nz - 1)],
-                device_id=(chip(y, zmod(z + dz), x), c), device_id_type=MESH,
-            ).start()
-
-    far_away = sorted(range(2, g.nz - 1), key=lambda v: -min(v, g.nz - v))
+            n, done = hops(j, way), passed.get((j, way), 0)
+            if j == 0:
+                go = done < n
+            elif kind == "combine":
+                go = g.at((1 - 2 * way) * n) >= g.tiers[1][3]
+            elif kind == "add":
+                go = done < n - 1
+            else:
+                go = True
+            if go:
+                rs_next(j, way)
 
     def swap(j):
         span = pl.ds(pl.multiple_of(c * g.dh + g.cuts[j], LANES), g.widths[j])
@@ -489,15 +519,9 @@
 
     def rs_last(j):
         total = own_part(j, 0)
-        if j in g.direct:
-            for n, some in enumerate((pl.ds(1, g.nz - 3), pl.ds(0, 1), pl.ds(g.nz - 2, 1))):
-                pltpu.make_async_copy(rrecv[j].at[some], rrecv[j].at[some], rs_recv.at[j, n]).wait()
-            for n in range(g.nz - 1):
-                total = total + rrecv[j][n].astype(F32)
-        else:
-            for way in range(2):
-                rs_copy(j, way, hops(j, way)).wait_recv()
-                total = total + rrecv[j][spot(j, way, hops(j, way))].astype(F32)
+        for way in range(2):
+            rs_copy(j, way, hops(j, way)).wait_recv()
+            total = total + rrecv[j][spot(j, way, hops(j, way))].astype(F32)
         if j:
             out_ref[:, pl.ds(pl.multiple_of(c * g.dh + g.cuts[j], LANES), g.widths[j])] = total.astype(BF16)
             swap(j).start()
@@ -510,27 +534,23 @@
                 one = jnp.where(expert_at == ids_ref[k:k + 1, :], scores, 0.0)
                 gate_ref[k:k + 1, :] = jnp.sum(one, axis=0, keepdims=True)
 
-    for kind, j, *step in sum_plan(g.widths, g.nz // 2, g.direct, g.early / g.slots):
+    for kind, j, *_ in sum_plan(g.widths, g.nz // 2):
         if kind == "make":
             make(j)
+        elif kind == "middle":
+            send_back(j, tier_rows(1), mid_recv.at[j])
         elif kind == "near":
-            send_back(j, early_rows, back_recv.at[j])
-        elif kind == "combine":
-            combine(j)
-            if j in g.direct:
-                rs_direct(j, far_away, 0)
-            else:
-                rs_step(j, 1, False)
-        elif kind == "add":
-            rs_step(j, step[0] + 1, False)
-        elif kind == "close":
-            combine_near(j)
-            if j in g.direct:
-                rs_direct(j, (1, g.nz - 1), 1)
-            else:
-                rs_step(j, 0, True)
+            send_back(j, tier_rows(0), back_recv.at[j])
+        elif kind == "last":
+            rs_last(j)
         else:
-            rs_last(j)
+            if kind == "combine":
+                combine(j)
+            elif kind == "mid":
+                combine_more(j, mid_t, 1, mid_recv.at[j])
+            elif kind == "close":
+                combine_more(j, near_t, 0, back_recv.at[j])
+            rs_move(j, kind)
 
     def gone(ref, sem):
         pltpu.make_async_copy(ref, ref, sem).wait()
@@ -573,8 +593,7 @@
         vm((g.all_slots, g.col), BF16),
         vm((g.all_slots, g.col), BF16),
         vm((g.col, g.all_slots), BF16),
-        vm((g.reach * g.tok, g.xy * g.early), BF16),
-        vm((g.col - (g.reach - 1) * g.tok, g.xy * (g.slots - g.early)), BF16),
+        *[vm(((last - first) * g.tok, g.xy * (high - low)), BF16) for low, high, first, last in g.tiers],
         vm((g.xy, g.slots, g.dim), BF16),
         vm((2, g.src, g.slots, g.dim), BF16),
         vm((g.dim, g.ff), BF16),
@@ -591,12 +610,13 @@
         dma((3,)),
         dma((3,)),
         dma(()),
-        dma(()),
+        dma((2,)),
         dma(()),
         dma((g.nq, 2, half)),
         dma(()),
         dma((2, len(g.near))),
         dma((2, g.nq)),
+        dma((g.nj,)),
         dma((g.nj,)),
         dma((g.nj,)),
         dma((g.nj,)),
@@ -612,10 +632,10 @@
     ]
 
 
-def per_device(ny, nz, nx, ahead, near, widths, direct, tokens, cotangent, expert_ids, gate_weights, w_gate, w_up, w_down):
+def per_device(ny, nz, nx, ahead, near, widths, tokens, cotangent, expert_ids, gate_weights, w_gate, w_up, w_down):
     tok, dim = tokens.shape
     top = expert_ids.shape[1]
-    g = Sizes(tok, dim, w_gate.shape[2], top, ny, nz, nx, ahead, near, widths, direct)
+    g = Sizes(tok, dim, w_gate.shape[2], top, ny, nz, nx, ahead, near, widths)
     vmem = pl.BlockSpec(memory_space=pltpu.VMEM)
     hbm = pl.BlockSpec(memory_space=pl.ANY)
     input_grad, gate_grad = pl.pallas_call(
@@ -634,7 +654,7 @@
     return input_grad, gate_grad.T.astype(BF16)
 
 
-def solution(mesh, ny=NY, nz=NZ, nx=NX, ahead=(256,) * 8, near=((0,), (1,), (2, 3), (4, 5), (6, 7)), widths=(LANES, 256, 256, 256, 256), direct=()):
+def solution(mesh, ny=NY, nz=NZ, nx=NX, ahead=(256,) * 8, near=((0,), (1,), (2, 3), (4, 5), (6, 7)), widths=(LANES, 256, 256, 256, 256)):
     placed = (
         P("expert", None),
         P("expert", None),
@@ -645,7 +665,7 @@
         P("expert", "half", None),
     )
     return jax.shard_map(
-        functools.partial(per_device, ny, nz, nx, ahead, near, widths, direct),
+        functools.partial(per_device, ny, nz, nx, ahead, near, widths),
         mesh=mesh,
         in_specs=placed,
         out_specs=(P("expert", None), P("expert", None)),

time: 89.4 us -> 86.5 us (0.968)
  Pallas kernels: 87.4 us -> 84.5 us
    pallas_call x1, Pallas kernels: 87.4 us -> 84.5 us  [per_device(): pl.pallas_call(functools.partial(kernel, g), out_shape=(pltpu.VMEM((tok,...]
where the time goes in v4:
time: 86.5 us; the launch traced here: 86.4 us
  Pallas kernels  84.5 us (98%)
    pallas_call x1, Pallas kernels, per_device(): pl.pallas_call(functools.partial(kernel, g), out_shape=(pltpu.VMEM((tok,...  84.5 us

profile of v4, /device:TPU:1, one launch (start us, length us, event | category | flops | bytes accessed | tf_op | source)
XLA Modules:
  0.0 86.4 jit_solution(11552147102089426973)
XLA Ops:
  0.6 84.5 %shard_map.86 = (bf16[64,2048]{1,0:T(8,128)(2,1)S(1)}, f32[8,64]{1,0:T(8,128)S(1)}) custom-call(s32[8,64]{1,0:T(8,128)} %bitcast.4, f32[8,64]{1,0:T(8,128)} %bitcast.5, bf16[64,2048]{1,0:T(8,128)(2,1)} %tok_hbm.1, bf16[64,2048]{1,0:T(8,128)(2,1)} %cot_hbm.1, bf16[1,2048,384]{2,1,0:T(8,128)(2,1)} %wg_hbm.1, bf16[1,2048,384]{2,1,0:T(8,128)(2,1)} %wu_hbm.1, ...), custom_call_target="tpu_custom_call" | custom-call | tf_op jit(solution)/shard_map/pallas_call | solution.py:641
  85.1 0.7 copy.10
  85.8 0.6 convert_bitcast_fusion

commit v5 on v4

--- a/solution.py
+++ b/solution.py
@@ -380,9 +380,9 @@
             uacc[...] = nn(rows, wu[feats, :])
             hacc[...] = nt(grads, wd[:, feats])
         else:
+            hacc[...] += nt(grads, wd[:, feats])
             gacc[...] += nn(rows, wg[feats, :])
             uacc[...] += nn(rows, wu[feats, :])
-            hacc[...] += nt(grads, wd[:, feats])
 
     for i in range(g.src):
         span = slice(i * g.slots, (i + 1) * g.slots)
@@ -654,7 +654,7 @@
     return input_grad, gate_grad.T.astype(BF16)
 
 
-def solution(mesh, ny=NY, nz=NZ, nx=NX, ahead=(256,) * 8, near=((0,), (1,), (2, 3), (4, 5), (6, 7)), widths=(LANES, 256, 256, 256, 256)):
+def solution(mesh, ny=NY, nz=NZ, nx=NX, ahead=(256,) * 8, near=((0,), (1,), (2,), (3,), (4, 5), (6, 7)), widths=(LANES, 256, 256, 256, 256)):
     placed = (
         P("expert", None),
         P("expert", None),

time: 86.5 us -> 86.5 us (level)
  no operation moved by 1% of the time
where the time goes in v5:
time: 86.5 us; the launch traced here: 86.4 us
  Pallas kernels  84.5 us (98%)
    pallas_call x1, Pallas kernels, per_device(): pl.pallas_call(functools.partial(kernel, g), out_shape=(pltpu.VMEM((tok,...  84.5 us

profile of v5, /device:TPU:1, one launch (start us, length us, event | category | flops | bytes accessed | tf_op | source)
XLA Modules:
  0.0 86.4 jit_solution(14251919797353964548)
XLA Ops:
  0.6 84.5 %shard_map.86 = (bf16[64,2048]{1,0:T(8,128)(2,1)S(1)}, f32[8,64]{1,0:T(8,128)S(1)}) custom-call(s32[8,64]{1,0:T(8,128)} %bitcast.4, f32[8,64]{1,0:T(8,128)} %bitcast.5, bf16[64,2048]{1,0:T(8,128)(2,1)} %tok_hbm.1, bf16[64,2048]{1,0:T(8,128)(2,1)} %cot_hbm.1, bf16[1,2048,384]{2,1,0:T(8,128)(2,1)} %wg_hbm.1, bf16[1,2048,384]{2,1,0:T(8,128)(2,1)} %wu_hbm.1, ...), custom_call_target="tpu_custom_call" | custom-call | tf_op jit(solution)/shard_map/pallas_call | solution.py:641
  85.1 0.7 copy.10
  85.8 0.6 convert_bitcast_fusion
